TPU v7x, 32 devices: a whole 2x2x4 slice. The times are simulated.
32 devices in a mesh: facet: 4 (over z), pol: 4 (over y, x), tm: 2 (over core).
Axes of the slice: x: 2, y: 2, z: 4, core: 2. Of those that a mesh axis runs over, the one named last changes fastest.
Arguments:
- tile_spectral_lines: bfloat16 [64, 4, 2, 64, 4096], P('facet', 'pol', None, 'tm'), may hold values from -6 to 6
- taper_leading_axis: bfloat16 [4, 2, 128, 512], P('facet', 'tm'), may hold values from -0.25 to 0.25
- taper_trailing_axis: bfloat16 [4, 2, 128, 512], P('facet', 'tm'), may hold values from -0.25 to 0.25
- depth_layer_factors: bfloat16 [4, 2, 2, 128], P('facet', 'tm'), may hold values from -4 to 4
- measured_correlations: float32 [4, 8, 2, 128], P('facet', None, 'tm', 'pol'), may hold values from -6 to 6
- visibility_groups_table: int32 [4, 2, 3, 8], P('facet', 'tm'), may hold values from 0 to 130815, as said below
- antenna_links: int32 [2, 130816], replicated, may hold values from 0 to 511, as said below
- complex_receiver_factors: float32 [256, 4, 512], replicated, may hold values from -5 to 5
Outputs:
- residual: float32 [4, 8, 2, 128], P('facet', None, 'tm', 'pol')
- gain_grad: float32 [512, 1024], P(('facet', 'pol', 'tm'))
Inputs may be any that keep to these rules, and one draw needn't show every extreme that they name: `visibility_groups_table`: for each subgrid and owner, every block has a channel below 256, a count of 1 or more, and baselines offset to offset + count - 1 below 130816; the counts of one owner sum to at most 128, and some owner reaches 128 in every draw. `antenna_links`: each baseline joins two different stations.
All inputs are finite; a program needn't handle non-finite values.
Results may differ from a plain program's by a relative error of at most 0.012.
Values may be sent and summed in bfloat16 or wider, within the bound.
A program may use at most 192 MiB of HBM per device.

v0:
```python
import math

import jax
import jax.numpy as jnp
import numpy as np
from jax import lax
from jax.sharding import PartitionSpec as P

FGRID = 8
FS = 4096
MC = 64
SG = 512
NPOL = 4
NW = 2
NCH = 256
NST = 512


w_chirp = 0.37
grad_scale = 0.1
feed_first = np.array([0, 0, 1, 1])
feed_second = np.array([0, 1, 0, 1])


def dft_table(length):
    indices = jnp.arange(length, dtype=jnp.int32)
    product = indices[:, None] * indices[None, :] % length
    angles = 2.0 * math.pi / length * product.astype(jnp.float32)
    factor = 1.0 / math.sqrt(length)
    return (
        (jnp.cos(angles) * factor).astype(jnp.bfloat16),
        (jnp.sin(angles) * factor).astype(jnp.bfloat16),
    )


def phase_table(left_size, right_size, length):
    left_index = jnp.arange(left_size, dtype=jnp.int32)
    right_index = jnp.arange(right_size, dtype=jnp.int32)
    product = left_index[:, None] * right_index[None, :] % length
    angles = 2.0 * math.pi / length * product.astype(jnp.float32)
    return (jnp.cos(angles), -jnp.sin(angles))


def chirp_phase(row_total, side_cells):
    across = (jnp.arange(row_total, dtype=jnp.int32) - side_cells // 2).astype(jnp.float32)
    downward = (jnp.arange(side_cells, dtype=jnp.int32) - side_cells // 2).astype(jnp.float32)
    return (
        w_chirp
        * (across[:, None] * across[:, None] + downward[None, :] * downward[None, :])
        / float(side_cells * side_cells)
    )


def make_planes(sub_real, sub_imag, phase_grid, layers):
    planes_list = []
    for plane_index in range(layers):
        angles = 2.0 * math.pi * plane_index * phase_grid
        cosine = jnp.cos(angles)
        sine_part = jnp.sin(angles)
        planes_list.append(
            jnp.stack(
                [sub_real * cosine - sub_imag * sine_part, sub_real * sine_part + sub_imag * cosine]
            ).astype(jnp.bfloat16)
        )
    return jnp.stack(planes_list)


def decode_slots(block_table, slot_index):
    channels = block_table[..., 0, :]
    offsets = block_table[..., 1, :]
    amounts = block_table[..., 2, :]
    starts = jnp.cumsum(amounts, axis=-1) - amounts
    relative = slot_index[:, None] - starts[..., None, :]
    member = ((relative >= 0) & (relative < amounts[..., None, :])).astype(jnp.int32)
    slot_live = jnp.sum(member, axis=-1)
    channel = jnp.sum(member * channels[..., None, :], axis=-1)
    antenna_couple = jnp.sum(member * (offsets[..., None, :] + relative), axis=-1)
    return (slot_live, channel, antenna_couple)


def model_terms(pred_re, pred_im, obs_re, obs_im, gain_first, gain_second, slot_live):
    first_re = gain_first[..., 2 * feed_first]
    first_im = gain_first[..., 2 * feed_first + 1]
    second_re = gain_second[..., 2 * feed_second]
    second_im = gain_second[..., 2 * feed_second + 1]
    both_re = first_re * second_re + first_im * second_im
    both_im = first_im * second_re - first_re * second_im
    model_re = both_re * pred_re - both_im * pred_im
    model_im = both_re * pred_im + both_im * pred_re
    alive_mask = slot_live.astype(jnp.float32)[..., None]
    resid_re = alive_mask * (obs_re - model_re)
    resid_im = alive_mask * (obs_im - model_im)
    cross_re = second_re * pred_re + second_im * pred_im
    cross_im = second_im * pred_re - second_re * pred_im
    lead_re = -(resid_re * cross_re - resid_im * cross_im)
    lead_im = -(resid_re * cross_im + resid_im * cross_re)
    along_re = first_re * pred_re - first_im * pred_im
    along_im = first_re * pred_im + first_im * pred_re
    trail_re = -(resid_re * along_re + resid_im * along_im)
    trail_im = -(resid_re * along_im - resid_im * along_re)
    leading = jnp.stack(
        [
            lead_re[..., 0] + lead_re[..., 1],
            lead_im[..., 0] + lead_im[..., 1],
            lead_re[..., 2] + lead_re[..., 3],
            lead_im[..., 2] + lead_im[..., 3],
        ],
        axis=-1,
    )
    trailing = jnp.stack(
        [
            trail_re[..., 0] + trail_re[..., 2],
            trail_im[..., 0] + trail_im[..., 2],
            trail_re[..., 1] + trail_re[..., 3],
            trail_im[..., 1] + trail_im[..., 3],
        ],
        axis=-1,
    )
    return (resid_re, resid_im, leading, trailing)


def degrid_block(layers, rows_u, rows_v, weights_w):
    spread_v = jnp.einsum("wcuv,nv->wcun", layers, rows_v, preferred_element_type=jnp.float32)
    along_u = jnp.sum(spread_v * jnp.transpose(rows_u).astype(jnp.float32)[None, None], axis=2)
    return jnp.sum(along_u * weights_w.astype(jnp.float32)[:, None, :], axis=0)


def on_device(
    tile_spectral_lines,
    taper_leading_axis,
    taper_trailing_axis,
    depth_layer_factors,
    measured_correlations,
    visibility_groups_table,
    antenna_links,
    complex_receiver_factors,
):
    careful = lax.Precision.HIGH
    facet_total = tile_spectral_lines.shape[0]
    row_share = tile_spectral_lines.shape[3]
    spread = FS // MC
    subgrids = lax.axis_size("facet")
    source = (
        tile_spectral_lines[:, 0].astype(jnp.float32).reshape(facet_total, 2, row_share, MC, spread)
    )
    source_re = source[:, 0]
    source_im = source[:, 1]
    inner_re, inner_im = phase_table(MC, MC, MC)
    section_re = jnp.einsum("fmar,ak->fmkr", source_re, inner_re, precision=careful) - jnp.einsum(
        "fmar,ak->fmkr", source_im, inner_im, precision=careful
    )
    section_im = jnp.einsum("fmar,ak->fmkr", source_re, inner_im, precision=careful) + jnp.einsum(
        "fmar,ak->fmkr", source_im, inner_re, precision=careful
    )
    twist_re, twist_im = phase_table(MC, spread, FS)
    turned_re = section_re * twist_re - section_im * twist_im
    turned_im = section_re * twist_im + section_im * twist_re
    outer_re, outer_im = phase_table(spread, subgrids, spread)
    factor = 1.0 / math.sqrt(FS)
    contrib_re = (
        jnp.einsum("fmkr,rs->sfmk", turned_re, outer_re, precision=careful)
        - jnp.einsum("fmkr,rs->sfmk", turned_im, outer_im, precision=careful)
    ) * factor
    contrib_im = (
        jnp.einsum("fmkr,rs->sfmk", turned_re, outer_im, precision=careful)
        + jnp.einsum("fmkr,rs->sfmk", turned_im, outer_re, precision=careful)
    ) * factor
    contrib = jnp.concatenate([contrib_re, contrib_im], axis=-1).astype(jnp.bfloat16)
    table_re, table_im = dft_table(SG)
    upper_half = jnp.concatenate([table_re, table_im], axis=1).reshape(FGRID, MC, 2 * SG)
    lower_half = jnp.concatenate([-table_im, table_re], axis=1).reshape(FGRID, MC, 2 * SG)
    stacked_table = jnp.stack([upper_half, lower_half], axis=1).reshape(FGRID, 2 * MC, 2 * SG)
    received = lax.all_to_all(contrib, "facet", split_axis=0, concat_axis=1, tiled=True)
    pieces = received.reshape(FGRID, FGRID, received.shape[2], 2 * MC)
    product = jnp.einsum("ijmc,jcv->imv", pieces, stacked_table, preferred_element_type=jnp.float32)
    half_rows = product.astype(jnp.bfloat16)
    whole_rows = lax.all_gather(half_rows, "tm", axis=1, tiled=True).reshape(SG, 2 * SG)
    owners = lax.axis_size("tm")
    owner_index = lax.axis_index("tm")
    row_count = SG // owners
    slots_own = taper_leading_axis.shape[2]
    flat_u = taper_leading_axis.reshape(slots_own, SG)
    flat_v = taper_trailing_axis.reshape(slots_own, SG)
    flat_w = depth_layer_factors.reshape(NW, slots_own)
    first_row = owner_index * row_count
    part_re = lax.dynamic_slice_in_dim(table_re, first_row, row_count, 0)
    part_im = lax.dynamic_slice_in_dim(table_im, first_row, row_count, 0)
    upper_rows = jnp.dot(part_re, whole_rows, preferred_element_type=jnp.float32)
    lower_rows = jnp.dot(part_im, whole_rows, preferred_element_type=jnp.float32)
    sub_real = upper_rows[:, :SG] - lower_rows[:, SG:]
    sub_imag = upper_rows[:, SG:] + lower_rows[:, :SG]
    own_part = jnp.stack([sub_real, sub_imag]).astype(jnp.bfloat16)
    subgrid = lax.all_gather(own_part, "tm", axis=1, tiled=True)
    layers = make_planes(subgrid[0], subgrid[1], chirp_phase(SG, SG), NW)
    predicted = degrid_block(layers, flat_u, flat_v, flat_w)
    regrouped = lax.all_to_all(predicted[None], "pol", split_axis=2, concat_axis=0, tiled=True)
    quarter = regrouped.shape[2]
    slot_index = lax.axis_index("pol") * quarter + jnp.arange(quarter, dtype=jnp.int32)
    slot_live, channel, antenna_couple = decode_slots(
        visibility_groups_table.reshape(3, visibility_groups_table.shape[3]), slot_index
    )
    antenna_left = jnp.take(antenna_links[0], antenna_couple)
    antenna_right = jnp.take(antenna_links[1], antenna_couple)
    gains_turned = jnp.transpose(complex_receiver_factors, (0, 2, 1))
    gain_first = gains_turned[channel, antenna_left]
    gain_second = gains_turned[channel, antenna_right]
    pred_re = jnp.transpose(regrouped[:, 0])
    pred_im = jnp.transpose(regrouped[:, 1])
    observed_local = measured_correlations.reshape(NPOL, 2, quarter)
    obs_re = jnp.transpose(observed_local[:, 0])
    obs_im = jnp.transpose(observed_local[:, 1])
    resid_re, resid_im, leading, trailing = model_terms(
        pred_re, pred_im, obs_re, obs_im, gain_first, gain_second, slot_live
    )
    residual = jnp.stack([jnp.transpose(resid_re), jnp.transpose(resid_im)], axis=1).reshape(
        1, 2 * NPOL, 1, quarter
    )
    channel_ids = jnp.arange(NCH, dtype=jnp.int32)
    own_count = NST // lax.axis_size(("facet", "pol", "tm"))
    own_stations = (
        lax.axis_index(("facet", "pol", "tm")) * own_count + jnp.arange(own_count, dtype=jnp.int32)
    ).astype(jnp.float32)
    channel_float = channel_ids.astype(jnp.float32)
    ident_rows = jnp.stack([antenna_left, antenna_right, channel]).astype(jnp.float32)
    records = jnp.concatenate([ident_rows, jnp.transpose(leading), jnp.transpose(trailing)], axis=0)
    piece = lax.all_gather(records, ("facet", "pol", "tm"), axis=1, tiled=True)
    piece_rows = piece.shape[1]
    group = math.gcd(piece_rows, 8 * quarter)
    grouped = jnp.transpose(piece.reshape(11, piece_rows // group, group), (1, 0, 2))

    def one_group(carry, record_block):
        match_first = (record_block[0][:, None] == own_stations[None, :]).astype(jnp.float32)
        match_second = (record_block[1][:, None] == own_stations[None, :]).astype(jnp.float32)
        weighted = (
            match_first[:, :, None] * jnp.transpose(record_block[3:7])[:, None, :]
            + match_second[:, :, None] * jnp.transpose(record_block[7:11])[:, None, :]
        )
        onehot = (record_block[2][:, None] == channel_float[None, :]).astype(jnp.float32)
        added = jnp.dot(
            jnp.transpose(weighted.reshape(group, own_count * 4)), onehot, precision=careful
        )
        return (carry + added.reshape(own_count, 4, NCH), None)

    result, unused = lax.scan(one_group, jnp.zeros((own_count, 4, NCH), jnp.float32), grouped)
    gain_grad = grad_scale * jnp.transpose(result, (0, 2, 1)).reshape(own_count, 4 * NCH)
    return (residual, gain_grad)


def solution(mesh):
    return jax.shard_map(
        on_device,
        mesh=mesh,
        in_specs=(
            P("facet", "pol", None, "tm", None),
            P("facet", "tm", None, None),
            P("facet", "tm", None, None),
            P("facet", "tm", None, None),
            P("facet", None, "tm", "pol"),
            P("facet", "tm", None, None),
            P(),
            P(),
        ),
        out_specs=(P("facet", None, "tm", "pol"), P(("facet", "pol", "tm"), None)),
        check_vma=False,
    )
```

profile of v0, /device:TPU:0, one launch (start us, length us, event | category | flops | bytes accessed | tf_op | source)
XLA Modules:
  0.0 357.3 jit_solution(9925717930749010015)
XLA Ops:
  7.2 7.8 %copy.78 = bf16[16,1,2,32,4096]{4,3,0,2,1:T(8,128)(2,1)} copy(bf16[16,1,2,32,4096]{4,3,2,1,0:T(8,128)(2,1)} %param.20) | data formatting | bytes 16777216 | tf_op args[0]
  15.0 23.6 %reshape.603 = bf16[16,2,32,64,64]{4,3,2,0,1:T(8,128)(2,1)} reshape(bf16[16,1,2,32,4096]{4,3,0,2,1:T(8,128)(2,1)} %copy.78) | data formatting | bytes 16777216 | tf_op jit(solution)/shard_map/reshape | solution.py:144
  38.5 13.9 %fusion.18 = f32[64,16,32,64]{3,0,2,1:T(8,128)} fusion(bf16[16,2,32,64,64]{4,3,2,0,1:T(8,128)(2,1)} %reshape.603), kind=kOutput, calls=%fused_computation.43 | convolution fusion | flops 805363712 | bytes 16777216 | tf_op jit(solution)/shard_map/fmar,ak->fmkr/dot_general | solution.py:149
  52.4 8.6 %fusion.17 = f32[64,16,32,64]{3,0,2,1:T(8,128)} fusion(bf16[16,2,32,64,64]{4,3,2,0,1:T(8,128)(2,1)S(1)} %copy-done.1), kind=kOutput, calls=%fused_computation.42 | convolution fusion | flops 805367808 | bytes 16777216 | tf_op jit(solution)/shard_map/fmar,ak->fmkr/dot_general | solution.py:152
  61.3 18.6 %convolution_subtract_fusion = f32[64,16,32,64]{3,0,2,1:T(8,128)} fusion(f32[64,16,32,64]{3,0,2,1:T(8,128)} %fusion.18, bf16[16,2,32,64,64]{4,3,2,0,1:T(8,128)(2,1)} %reshape.603), kind=kOutput, calls=%fused_computation.39 | convolution fusion | flops 807464960 | bytes 33554432 | tf_op jit(solution)/shard_map/fmar,ak->fmkr/dot_general | solution.py:149
  79.8 18.6 %convolution_add_fusion.1 = f32[64,16,32,64]{3,0,2,1:T(8,128)} fusion(f32[64,16,32,64]{3,0,2,1:T(8,128)} %fusion.17, bf16[16,2,32,64,64]{4,3,2,0,1:T(8,128)(2,1)} %reshape.603), kind=kOutput, calls=%fused_computation.38 | convolution fusion | flops 807460864 | bytes 33554432 | tf_op jit(solution)/shard_map/fmar,ak->fmkr/dot_general | solution.py:152
  98.6 25.9 %fusion.11 = f32[4,16,32,64]{3,0,2,1:T(4,128)S(1)} fusion(f32[64,16,32,64]{3,0,2,1:T(8,128)} %convolution_add_fusion.1, f32[64,16,32,64]{3,0,2,1:T(8,128)} %convolution_subtract_fusion, f32[64,64]{1,0:T(8,128)S(1)} %copy.80, f32[64,64]{1,0:T(8,128)S(1)} %copy.79), kind=kOutput, calls=%fused_computation.30 | convolution fusion | flops 56626944 | bytes 17334272 | tf_op jit(solution)/shard_map/fmkr,rs->sfmk/dot_general | solution.py:162
  124.5 25.5 %fusion.9 = f32[4,16,32,64]{3,0,2,1:T(4,128)S(1)} fusion(f32[64,16,32,64]{3,0,2,1:T(8,128)} %convolution_add_fusion.1, f32[64,16,32,64]{3,0,2,1:T(8,128)} %convolution_subtract_fusion, f32[64,64]{1,0:T(8,128)S(1)} %copy.80, f32[64,64]{1,0:T(8,128)S(1)} %copy.79), kind=kOutput, calls=%fused_computation.28 | convolution fusion | flops 56626688 | bytes 17334272 | tf_op jit(solution)/shard_map/fmkr,rs->sfmk/dot_general | solution.py:166
  150.0 25.7 %fusion.41 = bf16[4,16,32,64]{3,0,2,1:T(4,128)(2,1)S(1)} fusion(f32[4,16,32,64]{3,0,2,1:T(4,128)S(1)} %fusion.11, f32[64,16,32,64]{3,0,2,1:T(8,128)} %convolution_add_fusion.1, f32[64,64]{1,0:T(8,128)S(1)} %copy.80, f32[64,16,32,64]{3,0,2,1:T(8,128)} %convolution_subtract_fusion, f32[64,64]{1,0:T(8,128)S(1)} %copy.79), kind=kOutput, calls=%fused_computation.78 | convolution fusion | flops 57019904 | bytes 17596416 | tf_op jit(solution)/shard_map/fmkr,rs->sfmk/dot_general | solution.py:161
  175.7 25.7 %fusion.50 = bf16[4,16,32,64]{3,0,2,1:T(4,128)(2,1)S(1)} fusion(f32[4,16,32,64]{3,0,2,1:T(4,128)S(1)} %fusion.9, f32[64,16,32,64]{3,0,2,1:T(8,128)} %convolution_add_fusion.1, f32[64,64]{1,0:T(8,128)S(1)} %copy.80, f32[64,16,32,64]{3,0,2,1:T(8,128)} %convolution_subtract_fusion, f32[64,64]{1,0:T(8,128)S(1)} %copy.79), kind=kOutput, calls=%fused_computation.81 | convolution fusion | flops 57020160 | bytes 17596416 | tf_op jit(solution)/shard_map/fmkr,rs->sfmk/dot_general | solution.py:165
  201.4 0.7 pad_maximum_fusion
  202.2 0.9 copy.81
  203.0 6.3 %all-to-all-start = ((bf16[4,16,32,128]{3,2,1,0:T(8,128)(2,1)}), bf16[4,16,32,128]{3,2,1,0:T(8,128)(2,1)}, u32[]{:S(2)}, u32[]{:S(2)}) async-start(bf16[4,16,32,128]{3,2,1,0:T(8,128)(2,1)} %copy.81), calls=%async_computation | async-start | bytes 1048576 | tf_op jit(solution)/shard_map/all_to_all | solution.py:173
  209.4 4.9 %multiply_convert_fusion = (bf16[8,1,64,512]{3,2,1,0:T(8,128)(2,1)S(1)}, bf16[8,1,64,512]{3,2,1,0:T(8,128)(2,1)S(1)}) fusion(s32[8,64]{1,0:T(8,128)S(1)} %multiply_add_fusion.4), kind=kLoop, calls=%fused_computation.97 | loop fusion | flops 4718592 | bytes 1050624 | tf_op jit(solution)/shard_map/convert_element_type | solution.py:32
  214.3 4.9 %fusion.88 = bf16[8,1,64,512]{3,2,1,0:T(8,128)(2,1)} fusion(s32[8,64]{1,0:T(8,128)S(1)} %multiply_add_fusion.4), kind=kLoop, calls=%fused_computation.126 | loop fusion | flops 4980736 | bytes 526336 | tf_op jit(solution)/shard_map/neg | solution.py:171
  219.5 0.6 convert_reduce_fusion
  220.1 2.7 maximum_maximum_fusion
  222.7 4.1 %slice_reduce_fusion.1 = (s32[130816]{0:T(1024)S(1)}, s32[130816]{0:T(1024)S(1)}) fusion(s32[2,130816]{1,0:T(2,128)} %param.26), kind=kLoop, calls=%fused_computation.118 | loop fusion | bytes 2093056 | tf_op jit(solution)/shard_map/slice | solution.py:202
  226.9 3.3 fusion.34
  230.3 0.7 gather_fusion.6
  231.0 0.7 gather_fusion.7
  231.7 0.5 fusion.58
  232.2 0.5 fusion.168
  232.7 0.6 copy-done.7
  233.3 0.9 convert_bitcast_fusion
  234.2 6.6 %all-gather.4.cloned.1.call-done = bf16[8,64,1024]{2,1,0:T(8,128)(2,1)} async-done(((bf16[8,32,1024]{2,1,0:T(8,128)(2,1)}), bf16[8,64,1024]{2,1,0:T(8,128)(2,1)}) %all-gather.4.cloned.1.call-update) | async-done | bytes 1048592 | tf_op jit(solution)/shard_map/all_gather | solution.py:177
  240.8 3.2 fusion.82
  244.0 3.2 fusion.83
  247.3 0.3 fusion.84
  247.6 0.8 pad_maximum_fusion.1
  248.7 30.8 %copy.73 = f32[256,4,512]{1,2,0:T(8,128)} copy(f32[256,4,512]{2,1,0:T(4,128)S(1)} %copy-done.2) | data formatting | bytes 4194304 | tf_op args[7]
  279.5 1.7 gather_fusion
  281.2 0.6 gather_fusion.1
  281.8 0.6 gather_fusion.4
  282.4 1.6 gather_fusion.2
  284.2 9.7 %fusion.81 = (bf16[1,1,512,512]{3,2,1,0:T(8,128)(2,1)S(1)}, bf16[1,1,512,512]{3,2,1,0:T(8,128)(2,1)S(1)}, bf16[1,1,512,512]{3,2,1,0:T(8,128)(2,1)S(1)}, bf16[1,1,512,512]{3,2,1,0:T(8,128)(2,1)S(1)}) fusion(f32[512]{0:T(512)S(1)} %convert_multiply_fusion.8, bf16[2,512,512]{2,1,0:T(8,128)(2,1)} %all-gather.6.cloned.1.call-done), kind=kLoop, calls=%fused_computation.116 | loop fusion | flops 5505024 | bytes 3149824 | tf_op jit(solution)/shard_map/stack | solution.py:61
  293.9 0.7 fusion.53
  294.6 0.7 copy.83
  295.4 5.2 %all-to-all-start.1 = ((f32[1,2,128]{1,0,2:T(1,128)}), f32[1,2,128]{1,0,2:T(1,128)S(1)}, u32[]{:S(2)}, u32[]{:S(2)}) async-start(f32[1,2,128]{1,0,2:T(1,128)} %copy.83), calls=%async_computation.1 | async-start | bytes 131072 | tf_op jit(solution)/shard_map/all_to_all | solution.py:196
  300.7 0.6 gather_fusion.3
  301.2 0.6 gather_fusion.5
  301.8 3.6 %all-to-all-done.1 = f32[1,2,128]{1,0,2:T(1,128)S(1)} async-done(((f32[1,2,128]{1,0,2:T(1,128)}), f32[1,2,128]{1,0,2:T(1,128)S(1)}, u32[]{:S(2)}, u32[]{:S(2)}) %all-to-all-start.1) | async-done | bytes 1056 | tf_op jit(solution)/shard_map/all_to_all | solution.py:196
  305.7 40.3 %all-gather = f32[32,32,11]{1,2,0:T(8,128)S(1)} all-gather(f32[1,32,11]{1,2,0:T(8,128)S(1)} %maximum_bitcast_fusion), channel_id=1, replica_groups=mesh['facet'=4,'pol'=4,'tm'=2] {'facet','pol','tm'}, dimensions={0}, use_global_device_ids=true | all-gather | bytes 46464 | tf_op jit(solution)/shard_map/all_gather | solution.py:226
  346.2 2.1 while.11
  347.0 0.3 convolution_add_fusion.3
  347.5 0.3 convolution_add_fusion.3
  348.6 0.8 copy.91
  349.4 0.6 copy.86
  (123 shorter events, 3.1 us)
Async XLA Ops:
  7.2 286.7 %copy-start = (bf16[1,1,128,512]{3,2,1,0:T(8,128)(2,1)S(1)}, bf16[1,1,128,512]{3,2,1,0:T(8,128)(2,1)}, u32[]{:S(2)}) copy-start(bf16[1,1,128,512]{3,2,1,0:T(8,128)(2,1)} %param.22) | copy-start | bytes 393220
  38.5 13.9 %copy-start.1 = (bf16[16,2,32,64,64]{4,3,2,0,1:T(8,128)(2,1)S(1)}, bf16[16,2,32,64,64]{4,3,2,0,1:T(8,128)(2,1)}, u32[]{:S(2)}) copy-start(bf16[16,2,32,64,64]{4,3,2,0,1:T(8,128)(2,1)} %reshape.603) | copy-start | bytes 25165828
  175.7 43.6 %copy-start.11 = (s32[1,1,3,8]{3,1,2,0:T(1,128)S(1)}, s32[1,1,3,8]{3,1,2,0:T(1,128)}, u32[]{:S(2)}) copy-start(s32[1,1,3,8]{3,1,2,0:T(1,128)} %param.25) | copy-start | bytes 292
  201.4 30.3 %copy-start.15 = (s32[4]{0:T(128)S(1)}, s32[4]{0:T(128)}, u32[]{:S(2)}) copy-start(s32[4]{0:T(128)} %constant.192) | copy-start | bytes 52
  201.4 30.3 %copy-start.14 = (s32[4]{0:T(128)S(1)}, s32[4]{0:T(128)}, u32[]{:S(2)}) copy-start(s32[4]{0:T(128)} %constant.194) | copy-start | bytes 52
  201.4 47.2 %copy-start.2 = (f32[256,4,512]{2,1,0:T(4,128)S(1)}, f32[256,4,512]{2,1,0:T(4,128)}, u32[]{:S(2)}) copy-start(f32[256,4,512]{2,1,0:T(4,128)} %param.27) | copy-start | bytes 6291460
  203.0 23.8 %all-to-all-start = ((bf16[4,16,32,128]{3,2,1,0:T(8,128)(2,1)}), bf16[4,16,32,128]{3,2,1,0:T(8,128)(2,1)}, u32[]{:S(2)}, u32[]{:S(2)}) async-start(bf16[4,16,32,128]{3,2,1,0:T(8,128)(2,1)} %copy.81), calls=%async_computation | async-start | bytes 1048576 | tf_op jit(solution)/shard_map/all_to_all | solution.py:173
  209.4 31.4 %all-gather.4.cloned.1.call-start = ((), (), s32[]{:S(2)}) async-start(), calls=%async_computation.2 | async-start | bytes 1572864 | tf_op jit(solution)/shard_map/all_gather | solution.py:177
  220.1 12.7 %copy-start.3 = (s32[32]{0:T(128)}, s32[32]{0:T(128)S(1)}, u32[]{:S(2)}) copy-start(s32[32]{0:T(128)S(1)} %get-tuple-element.72) | copy-start | bytes 388
  230.2 54.0 %all-gather.6.cloned.1.call-start = ((), (), s32[]{:S(2)}) async-start(), calls=%async_computation.3 | async-start | bytes 1572864 | tf_op jit(solution)/shard_map/all_gather | solution.py:193
  231.7 1.1 copy-start.9
  232.7 0.6 copy-start.7
  248.6 35.4 %copy-start.8 = (pred[32]{0:T(512)(128)(4,1)S(1)}, pred[32]{0:T(512)(128)(4,1)}, u32[]{:S(2)}) copy-start(pred[32]{0:T(512)(128)(4,1)} %copy-done.7) | copy-start | bytes 100
  248.6 35.4 %copy-start.10 = (s32[32]{0:T(128)S(1)}, s32[32]{0:T(128)}, u32[]{:S(2)}) copy-start(s32[32]{0:T(128)} %copy-done.9) | copy-start | bytes 388
  248.6 35.4 %copy-start.4 = (s32[32]{0:T(128)S(1)}, s32[32]{0:T(128)}, u32[]{:S(2)}) copy-start(s32[32]{0:T(128)} %copy-done.3) | copy-start | bytes 388
  248.6 35.4 %copy-start.6 = (s32[1,32]{1,0:T(1,128)S(1)}, s32[1,32]{1,0:T(1,128)}, u32[]{:S(2)}) copy-start(s32[1,32]{1,0:T(1,128)} %get-tuple-element.82) | copy-start | bytes 388
  248.6 35.4 %copy-start.13 = (s32[4]{0:T(128)S(1)}, s32[4]{0:T(128)}, u32[]{:S(2)}) copy-start(s32[4]{0:T(128)} %constant.193) | copy-start | bytes 52
  248.7 35.5 %copy-start.12 = (s32[4]{0:T(128)S(1)}, s32[4]{0:T(128)}, u32[]{:S(2)}) copy-start(s32[4]{0:T(128)} %constant.195) | copy-start | bytes 52
  248.7 35.5 %copy-start.17 = (bf16[1,1,2,128]{3,2,1,0:T(2,128)(2,1)S(1)}, bf16[1,1,2,128]{3,2,1,0:T(2,128)(2,1)}, u32[]{:S(2)}) copy-start(bf16[1,1,2,128]{3,2,1,0:T(2,128)(2,1)} %param.23) | copy-start | bytes 1540
  248.7 35.5 %copy-start.5 = (f32[1,8,1,32]{3,2,1,0:T(1,128)S(1)}, f32[1,8,1,32]{3,2,1,0:T(1,128)}, u32[]{:S(2)}) copy-start(f32[1,8,1,32]{3,2,1,0:T(1,128)} %param.24) | copy-start | bytes 3076
  248.7 53.1 %copy-start.16 = (s32[32]{0:T(128)S(1)}, s32[32]{0:T(128)}, u32[]{:S(2)}) copy-start(s32[32]{0:T(128)} %get-tuple-element.71) | copy-start | bytes 388
  295.4 10.1 %all-to-all-start.1 = ((f32[1,2,128]{1,0,2:T(1,128)}), f32[1,2,128]{1,0,2:T(1,128)S(1)}, u32[]{:S(2)}, u32[]{:S(2)}) async-start(f32[1,2,128]{1,0,2:T(1,128)} %copy.83), calls=%async_computation.1 | async-start | bytes 131072 | tf_op jit(solution)/shard_map/all_to_all | solution.py:196
Sparse Core Ops, SparseCore 0:
  230.3 10.4 all-gather.3
  248.6 10.1 all-gather.5
where the time goes:
time: 364 us; the launch traced here: 357 us
  matrix products  174 us (48%)
  local copies, waits for them, and re-layouts  78.2 us (21%)
  blocking collectives  40.3 us (11%)
  other arithmetic  27.6 us (8%)
  between operations  15 us (4%)
  starting transfers between devices  11.6 us (3%)
  waiting for transfers between devices  10.2 us (3%)
    all_gather x1, blocking collectives, on_device(): piece = lax.all_gather(records, ('facet', 'pol', 'tm'), axis=1, tiled=True)  40.3 us
    unnamed x40, local copies, waits for them, and re-layouts  40.1 us
    dot_general x1, matrix products, on_device(): jnp.einsum('fmkr,rs->sfmk', turned_im, outer_im, precision=careful)  25.9 us
    dot_general x1, matrix products, on_device(): jnp.einsum('fmkr,rs->sfmk', turned_re, outer_im, precision=careful)  25.7 us
    dot_general x1, matrix products, on_device(): jnp.einsum('fmkr,rs->sfmk', turned_re, outer_re, precision=careful)  25.7 us
    dot_general x1, matrix products, on_device(): jnp.einsum('fmkr,rs->sfmk', turned_im, outer_re, precision=careful)  25.5 us
    reshape x1, local copies, waits for them, and re-layouts, on_device(): tile_spectral_lines[:, 0].astype(jnp.float32)  23.6 us
    dot_general x1, matrix products, on_device(): jnp.einsum('fmar,ak->fmkr', source_im, inner_re, precision=careful)  18.6 us
  transfers between devices with their start and end apart: 4, of which 2 were waited for; matrix products, arithmetic and copies ran while one was open for 16% of the time, Pallas kernels for 0%

commit v1 on v0

v1 whole, which is shorter than its diff:
```python
import functools
import math

import jax
import jax.numpy as jnp
import numpy as np
from jax import lax
from jax.experimental import pallas as pl
from jax.experimental.pallas import tpu as pltpu
from jax.sharding import PartitionSpec as P

FGRID = 8
FS = 4096
MC = 64
SG = 512
NPOL = 4
NW = 2
NCH = 256
NST = 512
CHUNK = 512

w_chirp = 0.37
grad_scale = 0.1
feed_first = np.array([0, 0, 1, 1])
feed_second = np.array([0, 1, 0, 1])


def unit_angles(left, right, length):
    product = np.outer(np.arange(left), np.arange(right)) % length
    return 2.0 * math.pi * product / length


def fourier_factors(subgrids):
    spread = FS // MC
    alpha = unit_angles(FS // spread, MC, MC)
    p = np.concatenate([np.cos(alpha), -np.sin(alpha)], axis=1) / math.sqrt(FS)
    q = np.concatenate([-np.sin(alpha), -np.cos(alpha)], axis=1) / math.sqrt(FS)
    beta = unit_angles(spread, subgrids * MC, FS).reshape(spread, subgrids, 1, MC)
    beta = np.broadcast_to(beta, (spread, subgrids, 2, MC)).reshape(spread, subgrids * 2 * MC)
    tile = lambda t: np.tile(t, (1, subgrids)).astype(np.float32)
    return (
        tile(p),
        tile(q),
        np.cos(beta).astype(np.float32),
        np.sin(beta).astype(np.float32),
    )


def fourier_kernel(p_ref, q_ref, c_ref, s_ref, x_ref, o_ref, table, total):
    step = pl.program_id(0)
    facets, _, rows, chunk = x_ref.shape
    subgrids = o_ref.shape[0]
    spread = c_ref.shape[0]
    cosine, sine = c_ref[...], s_ref[...]
    for part in range(chunk // spread):
        lead = p_ref[part : part + 1, :]
        other = q_ref[part : part + 1, :]
        table[part * spread : (part + 1) * spread, :] = (lead * cosine + other * sine).astype(
            jnp.bfloat16
        )
    x = x_ref[...].reshape(facets * 2 * rows, chunk)
    product = jnp.dot(x, table[...], preferred_element_type=jnp.float32)

    @pl.when(step == 0)
    def _():
        total[...] = product

    @pl.when(step > 0)
    def _():
        total[...] += product

    @pl.when(step == pl.num_programs(0) - 1)
    def _():
        lane = lax.broadcasted_iota(jnp.int32, (rows, 2 * MC), 1)
        sign = jnp.where(lane < MC, -1.0, 1.0)
        packed = o_ref.shape[3] // (2 * MC)
        for f in range(facets):
            for s in range(subgrids):
                cut = slice(s * 2 * MC, (s + 1) * 2 * MC)
                first = total[2 * f * rows : (2 * f + 1) * rows, cut]
                second = total[(2 * f + 1) * rows : (2 * f + 2) * rows, cut]
                value = first + sign * pltpu.roll(second, MC, 1)
                j = f % packed
                o_ref[s, f // packed, :, j * 2 * MC : (j + 1) * 2 * MC] = value.astype(jnp.bfloat16)


def fourier(x, subgrids):
    facets, _, rows, length = x.shape
    width = subgrids * 2 * MC
    spread = FS // MC
    packed = FGRID if facets % FGRID == 0 else 1
    per_step = CHUNK // spread
    factors = [jnp.asarray(t) for t in fourier_factors(subgrids)]
    return pl.pallas_call(
        fourier_kernel,
        out_shape=jax.ShapeDtypeStruct(
            (subgrids, facets // packed, rows, packed * 2 * MC), jnp.bfloat16
        ),
        grid=(length // CHUNK,),
        in_specs=[
            pl.BlockSpec((per_step, width), lambda g: (g, 0)),
            pl.BlockSpec((per_step, width), lambda g: (g, 0)),
            pl.BlockSpec((spread, width), lambda g: (0, 0)),
            pl.BlockSpec((spread, width), lambda g: (0, 0)),
            pl.BlockSpec((facets, 2, rows, CHUNK), lambda g: (0, 0, 0, g)),
        ],
        out_specs=pl.BlockSpec(
            (subgrids, facets // packed, rows, packed * 2 * MC), lambda g: (0, 0, 0, 0)
        ),
        scratch_shapes=[
            pltpu.VMEM((CHUNK, width), jnp.bfloat16),
            pltpu.VMEM((facets * 2 * rows, width), jnp.float32),
        ],
        compiler_params=pltpu.CompilerParams(
            dimension_semantics=("arbitrary",), vmem_limit_bytes=48 << 20
        ),
    )(*factors, x)


def subgrid_tables():
    angle = unit_angles(SG, SG, SG)
    re = np.cos(angle) / math.sqrt(SG)
    im = np.sin(angle) / math.sqrt(SG)
    blocks = lambda t: t.reshape(SG, FGRID, MC)
    second = np.stack([blocks(re), -blocks(im)], axis=2).reshape(SG, 2 * SG)
    third = np.stack([blocks(im), blocks(re)], axis=2).reshape(SG, 2 * SG)
    return [t.astype(jnp.bfloat16) for t in (re, im, second, third)]


def chirp_line():
    offset = np.arange(SG) - SG // 2
    angle = 2.0 * math.pi * w_chirp * (offset * offset) / float(SG * SG)
    return np.cos(angle).astype(np.float32), np.sin(angle).astype(np.float32)


def chirped(taper):
    cosine, sine = chirp_line()
    wide = taper.astype(jnp.float32)
    return jnp.concatenate(
        [taper, (wide * cosine).astype(jnp.bfloat16), (wide * sine).astype(jnp.bfloat16)], axis=0
    )


def decode_slots(block_table, slot_index):
    channels = block_table[0]
    offsets = block_table[1]
    amounts = block_table[2]
    starts = jnp.cumsum(amounts) - amounts
    relative = slot_index[:, None] - starts[None, :]
    member = ((relative >= 0) & (relative < amounts[None, :])).astype(jnp.int32)
    slot_live = jnp.sum(member, axis=-1)
    channel = jnp.sum(member * channels[None, :], axis=-1)
    baseline = jnp.sum(member * (offsets[None, :] + relative), axis=-1)
    return slot_live, channel, baseline, member


def model_terms(pred_re, pred_im, obs_re, obs_im, gain_first, gain_second, slot_live):
    first_re = gain_first[2 * feed_first]
    first_im = gain_first[2 * feed_first + 1]
    second_re = gain_second[2 * feed_second]
    second_im = gain_second[2 * feed_second + 1]
    both_re = first_re * second_re + first_im * second_im
    both_im = first_im * second_re - first_re * second_im
    model_re = both_re * pred_re - both_im * pred_im
    model_im = both_re * pred_im + both_im * pred_re
    alive_mask = slot_live.astype(jnp.float32)[None, :]
    resid_re = alive_mask * (obs_re - model_re)
    resid_im = alive_mask * (obs_im - model_im)
    cross_re = second_re * pred_re + second_im * pred_im
    cross_im = second_im * pred_re - second_re * pred_im
    lead_re = -(resid_re * cross_re - resid_im * cross_im)
    lead_im = -(resid_re * cross_im + resid_im * cross_re)
    along_re = first_re * pred_re - first_im * pred_im
    along_im = first_re * pred_im + first_im * pred_re
    trail_re = -(resid_re * along_re + resid_im * along_im)
    trail_im = -(resid_re * along_im - resid_im * along_re)
    leading = jnp.stack(
        [
            lead_re[0] + lead_re[1],
            lead_im[0] + lead_im[1],
            lead_re[2] + lead_re[3],
            lead_im[2] + lead_im[3],
        ]
    )
    trailing = jnp.stack(
        [
            trail_re[0] + trail_re[2],
            trail_im[0] + trail_im[2],
            trail_re[1] + trail_re[3],
            trail_im[1] + trail_im[3],
        ]
    )
    return resid_re, resid_im, leading, trailing


def nt_dot(left, right, **kw):
    return lax.dot_general(
        left, right, (((1,), (1,)), ((), ())), preferred_element_type=jnp.float32, **kw
    )


def on_device(
    tile_spectral_lines,
    taper_leading_axis,
    taper_trailing_axis,
    depth_layer_factors,
    measured_correlations,
    visibility_groups_table,
    antenna_links,
    complex_receiver_factors,
):
    exact = lax.Precision.HIGHEST
    subgrids = lax.axis_size("facet")
    owners = lax.axis_size("tm")
    pols = lax.axis_size("pol")
    owner_index = lax.axis_index("tm")
    slots = taper_leading_axis.shape[2]
    quarter = measured_correlations.shape[3]
    rows = tile_spectral_lines.shape[3]

    tapers = jnp.concatenate(
        [
            taper_leading_axis.reshape(slots, SG),
            taper_trailing_axis.reshape(slots, SG),
        ],
        axis=1,
    )
    partner = lax.ppermute(tapers, "tm", [(0, 1), (1, 0)])
    depth = depth_layer_factors.reshape(NW, slots)
    depth_partner = lax.ppermute(depth, "tm", [(0, 1), (1, 0)])
    both = jnp.concatenate([tapers, partner], axis=0)
    depth_both = jnp.concatenate([depth, depth_partner], axis=1).astype(jnp.float32)

    contrib = fourier(tile_spectral_lines[:, 0], subgrids)
    received = lax.all_to_all(contrib, "facet", split_axis=0, concat_axis=1, tiled=True)
    if received.shape[3] == 2 * SG:
        lines = received.reshape(FGRID * rows, 2 * SG)
    else:
        lines = jnp.transpose(
            received.reshape(FGRID, FGRID, rows, 2 * MC), (0, 2, 1, 3)
        ).reshape(FGRID * rows, 2 * SG)

    table_re, table_im, second, third = [jnp.asarray(t) for t in subgrid_tables()]
    own = 2 * slots
    trail3 = chirped(both[:, SG:])
    right_a = jnp.dot(trail3, second, preferred_element_type=jnp.float32).reshape(3, own, 2 * SG)
    right_b = jnp.dot(trail3, third, preferred_element_type=jnp.float32).reshape(3, own, 2 * SG)
    right = jnp.stack(
        [
            right_a[0],
            right_a[1] - right_b[2],
            right_b[0],
            right_b[1] + right_a[2],
        ]
    ).astype(jnp.bfloat16)
    lead3 = chirped(both[:, :SG])

    def own_rows(table):
        return lax.dynamic_index_in_dim(
            table.reshape(FGRID, owners, rows, SG), owner_index, 1, keepdims=False
        ).reshape(FGRID * rows, SG)

    left_re = nt_dot(own_rows(table_re), lead3).reshape(FGRID * rows, 3, own)
    left_im = nt_dot(own_rows(table_im), lead3).reshape(FGRID * rows, 3, own)
    lre = jnp.stack([left_re[:, 0], left_re[:, 1] - left_im[:, 2]], axis=1)
    lim = jnp.stack([left_im[:, 0], left_re[:, 2] + left_im[:, 1]], axis=1)
    spread = nt_dot(lines, right.reshape(4 * own, 2 * SG)).reshape(FGRID * rows, 2, 2, own)
    part_re = jnp.sum(jnp.sum(lre * spread[:, 0] - lim * spread[:, 1], axis=0) * depth_both, axis=0)
    part_im = jnp.sum(jnp.sum(lre * spread[:, 1] + lim * spread[:, 0], axis=0) * depth_both, axis=0)
    part = jnp.stack([part_re, part_im]).reshape(2, 2, pols, quarter)
    part = jnp.where(owner_index == 0, part, part[:, ::-1])
    outgoing = jnp.transpose(part, (2, 1, 0, 3)).reshape(pols * owners, 2 * quarter)
    incoming = lax.all_to_all(outgoing, ("pol", "tm"), split_axis=0, concat_axis=0, tiled=True)
    pred = jnp.sum(incoming.reshape(pols, owners, 2, quarter), axis=1)

    slot_index = lax.axis_index("pol") * quarter + jnp.arange(quarter, dtype=jnp.int32)
    block_table = visibility_groups_table.reshape(3, visibility_groups_table.shape[3])
    slot_live, channel, baseline, member = decode_slots(block_table, slot_index)
    stations = jnp.take(antenna_links, baseline, axis=1)
    channel_gains = jnp.take(complex_receiver_factors, block_table[0], axis=0)
    blocks = block_table.shape[1]
    pick = (
        stations.reshape(2 * quarter)[:, None] == jnp.arange(NST, dtype=jnp.int32)[None, :]
    ).astype(jnp.float32)
    gains = nt_dot(channel_gains.reshape(blocks * 4, NST), pick, precision=exact)
    gains = gains.reshape(blocks, 4, 2, quarter)
    weight = jnp.transpose(member).astype(jnp.float32)[:, None, None, :]
    gains = jnp.sum(gains * weight, axis=0)
    observed = measured_correlations.reshape(NPOL, 2, quarter)
    resid_re, resid_im, leading, trailing = model_terms(
        pred[:, 0], pred[:, 1], observed[:, 0], observed[:, 1], gains[:, 0], gains[:, 1], slot_live
    )
    residual = jnp.stack([resid_re, resid_im], axis=1).reshape(1, 2 * NPOL, 1, quarter)

    everyone = ("facet", "pol", "tm")
    total = lax.axis_size(everyone)
    idents = jnp.concatenate([stations, channel[None]], axis=0).astype(jnp.float32)
    records = jnp.concatenate([idents, leading, trailing], axis=0).reshape(1, 11 * quarter)
    sent = jnp.broadcast_to(records, (total, 11 * quarter))
    piece = lax.all_to_all(sent, everyone, split_axis=0, concat_axis=0, tiled=True)
    piece = jnp.transpose(piece.reshape(total, 11, quarter), (1, 0, 2)).reshape(11, total * quarter)
    own_count = NST // total
    mine = (
        lax.axis_index(everyone) * own_count + jnp.arange(own_count, dtype=jnp.int32)
    ).astype(jnp.float32)
    match_first = (mine[:, None] == piece[0][None, :]).astype(jnp.float32)
    match_second = (mine[:, None] == piece[1][None, :]).astype(jnp.float32)
    weighted = match_first[:, None, :] * piece[None, 3:7] + match_second[:, None, :] * piece[None, 7:11]
    onehot = (
        jnp.arange(NCH, dtype=jnp.int32).astype(jnp.float32)[:, None] == piece[2][None, :]
    ).astype(jnp.float32)
    summed = nt_dot(
        weighted.reshape(own_count * 4, total * quarter), onehot, precision=lax.Precision.HIGH
    )
    gain_grad = grad_scale * jnp.transpose(
        summed.reshape(own_count, 4, NCH), (0, 2, 1)
    ).reshape(own_count, 4 * NCH)
    return residual, gain_grad


def solution(mesh):
    return jax.shard_map(
        on_device,
        mesh=mesh,
        in_specs=(
            P("facet", "pol", None, "tm", None),
            P("facet", "tm", None, None),
            P("facet", "tm", None, None),
            P("facet", "tm", None, None),
            P("facet", None, "tm", "pol"),
            P("facet", "tm", None, None),
            P(),
            P(),
        ),
        out_specs=(P("facet", None, "tm", "pol"), P(("facet", "pol", "tm"), None)),
        check_vma=False,
    )
```

time: 364 us -> 95.6 us (0.26); the launches traced: 357 us -> 94.6 us
  matrix products: 174 us -> 6 us
  blocking collectives: 40.3 us -> 0 us
  local copies, waits for them, and re-layouts: 78.2 us -> 44.3 us
  other arithmetic: 27.6 us -> 7.82 us
  between operations: 15 us -> 1.13 us
  Pallas kernels: 0 us -> 10.9 us
  starting transfers between devices: 11.6 us -> 15.4 us
    dot_general x16 -> x7, matrix products: 174 us -> 6 us  [the longest x5 4.04 us: nt_dot(): lax.dot_general(left, right, (((1,), (1,)), ((), ())), preferred_element_...]
    all_gather x1 -> x0, blocking collectives: 40.3 us -> none  [on_device(): piece = lax.all_gather(records, ('facet', 'pol', 'tm'), axis=1, tiled=True)]
    reshape x2, local copies, waits for them, and re-layouts: 23.6 us -> 0.18 us  [the longest x1 0.1 us: on_device(): piece.reshape(total, 11, quarter)]
    another operation x9 -> x3, other arithmetic: 14.1 us -> 1.8 us  [the longest x1 1.61 us: on_device(): jnp.stack([right_a[0], right_a[1] - right_b[2], right_b[0], right_b[1] +...]
    pallas_call x0 -> x1, Pallas kernels: none -> 10.9 us  [fourier(): pl.pallas_call(fourier_kernel, out_shape=jax.ShapeDtypeStruct((subgrids,...]
    all_gather x2 -> x0, waiting for transfers between devices: 6.59 us -> none  [the longest x1 6.57 us: on_device(): lax.all_gather(half_rows, 'tm', axis=1, tiled=True).reshape(SG, 2 * SG)]
    convert_element_type x17 -> x7, other arithmetic: 6.21 us -> 0.36 us  [the longest x1 0.19 us: chirped(): (wide * cosine).astype(jnp.bfloat16)]
    all_to_all x1 -> x2, waiting for transfers between devices: 3.62 us -> 9.07 us  [the longest x1 6.71 us: on_device(): lax.all_to_all(sent, everyone, split_axis=0, concat_axis=0, tiled=True)]
  transfers between devices with their start and end apart: 4 -> 5, of which waited for: 2 -> 2; matrix products, arithmetic and copies ran while one was open for 16% -> 50% of each run, Pallas kernels for 0% -> 12%
where the time goes in v1:
time: 95.6 us; the launch traced here: 94.6 us
  local copies, waits for them, and re-layouts  44.3 us (46%)
  starting transfers between devices  15.4 us (16%)
  Pallas kernels  10.9 us (11%)
  waiting for transfers between devices  9.08 us (9%)
  other arithmetic  7.82 us (8%)
  matrix products  6 us (6%)
  between operations  1.13 us (1%)
    unnamed x41, local copies, waits for them, and re-layouts  35 us
    pallas_call x1, Pallas kernels, fourier(): pl.pallas_call(fourier_kernel, out_shape=jax.ShapeDtypeStruct((subgrids,...  10.9 us
    all_to_all x1, waiting for transfers between devices, on_device(): lax.all_to_all(sent, everyone, split_axis=0, concat_axis=0, tiled=True)  6.71 us
    all_to_all x1, starting transfers between devices, on_device(): lax.all_to_all(contrib, 'facet', split_axis=0, concat_axis=1, tiled=True)  5.86 us
    all_to_all x1, starting transfers between devices, on_device(): lax.all_to_all(sent, everyone, split_axis=0, concat_axis=0, tiled=True)  4.77 us
    all_to_all x1, starting transfers between devices, on_device(): lax.all_to_all(outgoing, ('pol', 'tm'), split_axis=0, concat_axis=0, tile...  4.04 us
    dot_general x5, matrix products, nt_dot(): lax.dot_general(left, right, (((1,), (1,)), ((), ())), preferred_element_...  4.04 us
    all_to_all x1, waiting for transfers between devices, on_device(): lax.all_to_all(outgoing, ('pol', 'tm'), split_axis=0, concat_axis=0, tile...  2.36 us
  transfers between devices with their start and end apart: 5, of which 2 were waited for; matrix products, arithmetic and copies ran while one was open for 50% of the time, Pallas kernels for 12%

profile of v1, /device:TPU:0, one launch (start us, length us, event | category | flops | bytes accessed | tf_op | source)
XLA Modules:
  0.0 94.6 jit_solution(6559991500535007624)
XLA Ops:
  0.6 1.8 %pad_maximum_fusion.8 = bf16[128,1024]{1,0:T(8,128)(2,1)} fusion(bf16[128,512]{1,0:T(8,128)(2,1)} %bitcast.139, bf16[128,512]{1,0:T(8,128)(2,1)} %bitcast.141), kind=kLoop, calls=%fused_computation.46 | loop fusion | flops 524288 | bytes 524288 | tf_op jit(solution)/shard_map/concatenate | solution.py:221
  2.5 0.5 collective-permute-start
  3.0 0.9 copy-done.1
  3.9 0.9 copy-done.2
  4.8 0.9 copy-done.3
  5.7 0.9 copy-done.4
  6.6 10.9 %shard_map.275 = bf16[4,2,32,1024]{3,2,1,0:T(8,128)(2,1)} custom-call(f32[64,512]{1,0:T(8,128)S(1)} %copy-done.4, f32[64,512]{1,0:T(8,128)S(1)} %copy-done.1, f32[64,512]{1,0:T(8,128)S(1)} %copy-done.2, f32[64,512]{1,0:T(8,128)S(1)} %copy-done.3, bf16[16,2,32,4096]{3,2,1,0:T(8,128)(2,1)} %bitcast.125), custom_call_target="tpu_custom_call" | custom-call | tf_op jit(solution)/shard_map/pallas_call | solution.py:94
  17.5 5.9 %all-to-all-start = ((bf16[4,2,32,1024]{3,2,1,0:T(8,128)(2,1)}), bf16[4,2,32,1024]{3,2,1,0:T(8,128)(2,1)S(1)}, u32[]{:S(2)}, u32[]{:S(2)}) async-start(bf16[4,2,32,1024]{3,2,1,0:T(8,128)(2,1)} %shard_map.275), calls=%async_computation | async-start | bytes 1048576 | tf_op jit(solution)/shard_map/all_to_all | solution.py:235
  23.4 0.2 collective-permute-start.1
  23.6 0.2 reduce-window.8
  24.0 30.3 %copy.202 = s32[2,130816]{0,1:T(8,128)} copy(s32[2,130816]{1,0:T(2,128)} %param.34) | data formatting | bytes 2093056 | tf_op args[6]
  54.3 1.4 %gather_fusion.1 = s32[32,2]{1,0:T(8,128)S(1)} fusion(s32[2,130816]{0,1:T(8,128)} %copy.202, s32[1024]{0:T(1024)S(1)} %get-tuple-element.81), kind=kCustom, calls=%fused_computation.1 | custom fusion | bytes 640 | tf_op jit(solution)/shard_map/jit(_take)/gather | solution.py:279
  55.9 0.6 gather_fusion
  56.5 0.4 fusion.1
  57.0 1.1 %constant_dynamic-slice_fusion = (bf16[8,1,32,512]{3,2,0,1:T(8,128)(2,1)S(1)}, bf16[8,1,32,512]{3,2,0,1:T(8,128)(2,1)S(1)}) fusion(bf16[8,2,32,512]{3,2,0,1:T(8,128)(2,1)} %constant.125, s32[]{:T(128)S(6)} %select_n.86, bf16[8,2,32,512]{3,2,0,1:T(8,128)(2,1)} %constant.124), kind=kLoop, calls=%fused_computation.136 | loop fusion | bytes 1048580 | tf_op jit(solution)/shard_map/jit(dynamic_index_in_dim)/dynamic_slice | solution.py:259
  58.2 1.1 %pad_maximum_fusion.3 = bf16[256,1024]{1,0:T(8,128)(2,1)S(1)} fusion(bf16[128,1024]{1,0:T(8,128)(2,1)} %collective-permute-done, bf16[128,512]{1,0:T(8,128)(2,1)S(1)} %bitcast.140, bf16[128,512]{1,0:T(8,128)(2,1)S(1)} %bitcast.142), kind=kLoop, calls=%fused_computation.35 | loop fusion | flops 1572864 | bytes 1048576 | tf_op jit(solution)/shard_map/concatenate | solution.py:231
  59.3 0.2 fusion.6
  59.5 1.0 %fusion.17 = f32[768,1024]{1,0:T(8,128)S(1)} fusion(bf16[512,1024]{1,0:T(8,128)(2,1)S(1)} %copy-done.6, bf16[256,512]{1,0:T(8,128)(2,1)S(1)} %get-tuple-element.46, bf16[256,512]{1,0:T(8,128)(2,1)S(1)} %get-tuple-element.41, bf16[256,512]{1,0:T(8,128)(2,1)S(1)} %get-tuple-element.45), kind=kOutput, calls=%fused_computation.43 | convolution fusion | flops 807665664 | bytes 4980736 | tf_op jit(solution)/shard_map/dot_general | solution.py:246
  60.5 0.2 copy-done.5
  60.7 1.0 %fusion.16 = f32[768,1024]{1,0:T(8,128)S(1)} fusion(bf16[512,1024]{1,0:T(8,128)(2,1)S(1)} %copy-done.5, bf16[256,512]{1,0:T(8,128)(2,1)S(1)} %get-tuple-element.46, bf16[256,512]{1,0:T(8,128)(2,1)S(1)} %get-tuple-element.41, bf16[256,512]{1,0:T(8,128)(2,1)S(1)} %get-tuple-element.45), kind=kOutput, calls=%fused_computation.42 | convolution fusion | flops 807665664 | bytes 4980736 | tf_op jit(solution)/shard_map/dot_general | solution.py:247
  61.7 0.2 fusion.10
  61.9 0.5 fusion.11
  62.5 1.6 %pad_maximum_fusion = bf16[4,256,1024]{2,1,0:T(8,128)(2,1)} fusion(bf16[1,256,1024]{2,1,0:T(8,128)(2,1)S(1)} %get-tuple-element.35, bf16[1,256,1024]{2,1,0:T(8,128)(2,1)S(1)} %get-tuple-element.74, bf16[1,256,1024]{2,1,0:T(8,128)(2,1)S(1)} %get-tuple-element.34, bf16[1,256,1024]{2,1,0:T(8,128)(2,1)S(1)} %get-tuple-element.73), kind=kLoop, calls=%fused_computation.6 | loop fusion | flops 3145728 | bytes 4194304 | tf_op jit(solution)/shard_map/stack | solution.py:248
  64.1 0.4 fusion.51
  64.5 0.4 fusion.52
  64.9 0.8 slice_subtract_fusion.1
  65.7 2.4 %fusion.53 = f32[256,2,2,256]{3,0,2,1:T(8,128)S(1)} fusion(bf16[256,1024,1,1]{1,0,3,2:T(8,128)(2,1)S(1)} %bitcast.129, bf16[2,2,256,1024]{3,2,1,0:T(8,128)(2,1)} %bitcast.126), kind=kOutput, calls=%fused_computation.151 | convolution fusion | flops 536870912 | bytes 3670016 | tf_op jit(solution)/shard_map/dot_general | solution.py:197
  68.1 0.2 add_reduce_fusion
  68.5 0.7 all_to_all.18
  69.2 4.0 %all-to-all-start.1 = ((f32[8,1,64]{2,1,0:T(1,128)}), f32[8,1,64]{2,1,0:T(1,128)S(1)}, u32[]{:S(2)}, u32[]{:S(2)}) async-start(f32[8,1,64]{2,1,0:T(1,128)} %bitcast.36), calls=%async_computation.1 | async-start | bytes 8192 | tf_op jit(solution)/shard_map/all_to_all | solution.py:273
  73.2 0.6 gather_fusion.3
  73.8 0.6 gather_fusion.5
  74.4 0.6 gather_fusion.2
  74.9 0.6 gather_fusion.4
  75.5 2.4 %all-to-all-done.1 = f32[8,1,64]{2,1,0:T(1,128)S(1)} async-done(((f32[8,1,64]{2,1,0:T(1,128)}), f32[8,1,64]{2,1,0:T(1,128)S(1)}, u32[]{:S(2)}, u32[]{:S(2)}) %all-to-all-start.1) | async-done | bytes 2080 | tf_op jit(solution)/shard_map/all_to_all | solution.py:273
  77.9 0.5 broadcast.226
  78.4 0.7 reduce.16
  79.4 0.6 broadcast_in_dim.68
  80.0 4.8 %all-to-all-start.2 = ((f32[32,1,352]{2,1,0:T(1,128)}), f32[32,1,352]{2,1,0:T(1,128)S(1)}, u32[]{:S(2)}, u32[]{:S(2)}) async-start(f32[32,1,352]{2,1,0:T(1,128)} %broadcast_in_dim.68), calls=%async_computation.2 | async-start | bytes 98304 | tf_op jit(solution)/shard_map/all_to_all | solution.py:300
  84.8 0.6 copy.210
  85.4 6.7 %all-to-all-done.2 = f32[32,1,352]{2,1,0:T(1,128)S(1)} async-done(((f32[32,1,352]{2,1,0:T(1,128)}), f32[32,1,352]{2,1,0:T(1,128)S(1)}, u32[]{:S(2)}, u32[]{:S(2)}) %all-to-all-start.2) | async-done | bytes 45088 | tf_op jit(solution)/shard_map/all_to_all | solution.py:300
  92.1 0.1 reduce.1
  92.2 0.1 reshape.455
  92.4 0.1 slice_reduce_fusion.2
  92.8 0.1 mul.331
  93.0 0.5 fusion
  93.6 0.2 copy.214
  93.8 0.8 copy.216
  (88 shorter events, 1.6 us)
Async XLA Ops:
  0.6 55.2 %copy-start = (f32[256,4,512]{2,1,0:T(4,128)S(1)}, f32[256,4,512]{2,1,0:T(4,128)}, u32[]{:S(2)}) copy-start(f32[256,4,512]{2,1,0:T(4,128)} %param.35) | copy-start | bytes 6291460
  2.5 55.7 %collective-permute-start = (bf16[128,1024]{1,0:T(8,128)(2,1)}, bf16[128,1024]{1,0:T(8,128)(2,1)}, u32[]{:S(2)}, u32[]{:S(2)}) collective-permute-start(bf16[128,1024]{1,0:T(8,128)(2,1)} %pad_maximum_fusion.8), channel_id=1, source_target_pairs={{0,1},{1,0},{2,3},{3,2},{4,5},{5,4},{6,7},{7,6},{8,9},{9,8},{10,11... | collective-permute-start | bytes 786440 | tf_op jit(solution)/shard_map/ppermute | solution.py:228
  3.0 0.9 copy-start.1
  3.9 0.9 copy-start.2
  4.8 0.9 copy-start.3
  5.7 0.9 copy-start.4
  6.6 16.7 %copy-start.14 = (bf16[1,1,2,128]{3,2,1,0:T(2,128)(2,1)S(1)}, bf16[1,1,2,128]{3,2,1,0:T(2,128)(2,1)}, u32[]{:S(2)}) copy-start(bf16[1,1,2,128]{3,2,1,0:T(2,128)(2,1)} %param.31) | copy-start | bytes 1540
  6.6 17.0 %copy-start.13 = (s32[1,1,3,8]{3,1,2,0:T(1,128)S(1)}, s32[1,1,3,8]{3,1,2,0:T(1,128)}, u32[]{:S(2)}) copy-start(s32[1,1,3,8]{3,1,2,0:T(1,128)} %param.33) | copy-start | bytes 292
  17.5 48.2 %all-to-all-start = ((bf16[4,2,32,1024]{3,2,1,0:T(8,128)(2,1)}), bf16[4,2,32,1024]{3,2,1,0:T(8,128)(2,1)S(1)}, u32[]{:S(2)}, u32[]{:S(2)}) async-start(bf16[4,2,32,1024]{3,2,1,0:T(8,128)(2,1)} %shard_map.275), calls=%async_computation | async-start | bytes 1048576 | tf_op jit(solution)/shard_map/all_to_all | solution.py:235
  23.4 44.9 %collective-permute-start.1 = (bf16[2,128]{1,0:T(2,128)(2,1)S(1)}, bf16[2,128]{1,0:T(2,128)(2,1)S(1)}, u32[]{:S(2)}, u32[]{:S(2)}) collective-permute-start(bf16[2,128]{1,0:T(2,128)(2,1)S(1)} %bitcast.156), channel_id=1, source_target_pairs={{0,1},{1,0},{2,3},{3,2},{4,5},{5,4},{6,7},{7,6},{8,9},{9,8},{10,11... | collective-permute-start | bytes 1544 | tf_op jit(solution)/shard_map/ppermute | solution.py:230
  24.0 33.0 %copy-start.17 = (s32[4]{0:T(128)S(1)}, s32[4]{0:T(128)}, u32[]{:S(2)}) copy-start(s32[4]{0:T(128)} %constant.126) | copy-start | bytes 52
  24.0 33.0 %copy-start.18 = (s32[4]{0:T(128)S(1)}, s32[4]{0:T(128)}, u32[]{:S(2)}) copy-start(s32[4]{0:T(128)} %constant.127) | copy-start | bytes 52
  24.0 33.0 %copy-start.15 = (s32[4]{0:T(128)S(1)}, s32[4]{0:T(128)}, u32[]{:S(2)}) copy-start(s32[4]{0:T(128)} %constant.128) | copy-start | bytes 52
  24.0 33.0 %copy-start.16 = (s32[4]{0:T(128)S(1)}, s32[4]{0:T(128)}, u32[]{:S(2)}) copy-start(s32[4]{0:T(128)} %constant.129) | copy-start | bytes 52
  24.0 34.1 %copy-start.10 = (f32[1,8,1,32]{3,2,1,0:T(1,128)S(1)}, f32[1,8,1,32]{3,2,1,0:T(1,128)}, u32[]{:S(2)}) copy-start(f32[1,8,1,32]{3,2,1,0:T(1,128)} %param.32) | copy-start | bytes 3076
  24.0 34.1 %copy-start.8 = (bf16[1,1,128,512]{3,2,1,0:T(8,128)(2,1)S(1)}, bf16[1,1,128,512]{3,2,1,0:T(8,128)(2,1)}, u32[]{:S(2)}) copy-start(bf16[1,1,128,512]{3,2,1,0:T(8,128)(2,1)} %param.30) | copy-start | bytes 393220
  24.0 34.1 %copy-start.9 = (bf16[1,1,128,512]{3,2,1,0:T(8,128)(2,1)S(1)}, bf16[1,1,128,512]{3,2,1,0:T(8,128)(2,1)}, u32[]{:S(2)}) copy-start(bf16[1,1,128,512]{3,2,1,0:T(8,128)(2,1)} %param.29) | copy-start | bytes 393220
  54.3 5.0 %copy-start.11 = (f32[512]{0:T(512)S(1)}, f32[512]{0:T(512)}, u32[]{:S(2)}) copy-start(f32[512]{0:T(512)} %constant.107.clone) | copy-start | bytes 6148
  54.3 5.0 %copy-start.12 = (f32[512]{0:T(512)S(1)}, f32[512]{0:T(512)}, u32[]{:S(2)}) copy-start(f32[512]{0:T(512)} %constant.108.clone) | copy-start | bytes 6148
  58.1 1.4 %copy-start.6 = (bf16[512,1024]{1,0:T(8,128)(2,1)S(1)}, bf16[512,1024]{1,0:T(8,128)(2,1)}, u32[]{:S(2)}) copy-start(bf16[512,1024]{1,0:T(8,128)(2,1)} %constant.105.clone) | copy-start | bytes 3145732
  59.5 1.2 %copy-start.5 = (bf16[512,1024]{1,0:T(8,128)(2,1)S(1)}, bf16[512,1024]{1,0:T(8,128)(2,1)}, u32[]{:S(2)}) copy-start(bf16[512,1024]{1,0:T(8,128)(2,1)} %constant.106.clone) | copy-start | bytes 3145732
  65.7 2.4 %copy-start.7 = (f32[256,1,256]{2,0,1:T(8,128)S(1)}, f32[256,1,256]{2,0,1:T(8,128)}, u32[]{:S(2)}) copy-start(f32[256,1,256]{2,0,1:T(8,128)} %get-tuple-element.39) | copy-start | bytes 786436
  69.2 8.7 %all-to-all-start.1 = ((f32[8,1,64]{2,1,0:T(1,128)}), f32[8,1,64]{2,1,0:T(1,128)S(1)}, u32[]{:S(2)}, u32[]{:S(2)}) async-start(f32[8,1,64]{2,1,0:T(1,128)} %bitcast.36), calls=%async_computation.1 | async-start | bytes 8192 | tf_op jit(solution)/shard_map/all_to_all | solution.py:273
  80.0 12.1 %all-to-all-start.2 = ((f32[32,1,352]{2,1,0:T(1,128)}), f32[32,1,352]{2,1,0:T(1,128)S(1)}, u32[]{:S(2)}, u32[]{:S(2)}) async-start(f32[32,1,352]{2,1,0:T(1,128)} %broadcast_in_dim.68), calls=%async_computation.2 | async-start | bytes 98304 | tf_op jit(solution)/shard_map/all_to_all | solution.py:300

commit v2 on v1

--- a/solution.py
+++ b/solution.py
@@ -276,7 +276,9 @@
     slot_index = lax.axis_index("pol") * quarter + jnp.arange(quarter, dtype=jnp.int32)
     block_table = visibility_groups_table.reshape(3, visibility_groups_table.shape[3])
     slot_live, channel, baseline, member = decode_slots(block_table, slot_index)
-    stations = jnp.take(antenna_links, baseline, axis=1)
+    stations = jnp.stack(
+        [jnp.take(antenna_links[0], baseline), jnp.take(antenna_links[1], baseline)]
+    )
     channel_gains = jnp.take(complex_receiver_factors, block_table[0], axis=0)
     blocks = block_table.shape[1]
     pick = (

time: 95.6 us -> 70.8 us (0.74)
  local copies, waits for them, and re-layouts: 44.3 us -> 20.4 us
    unnamed x41 -> x40, local copies, waits for them, and re-layouts: 35 us -> 4.73 us
    slice x0 -> x1, local copies, waits for them, and re-layouts: none -> 5.02 us  [on_device(): antenna_links[0]]
    gather x1 -> x2, local copies, waits for them, and re-layouts: 1.36 us -> 2.84 us  [the longest x1 2.14 us: on_device(): jnp.take(antenna_links[0], baseline)]
  transfers between devices with their start and end apart: 5 -> 5, of which waited for: 2 -> 2; matrix products, arithmetic and copies ran while one was open for 50% -> 33% of each run, Pallas kernels for 12% -> 16%
where the time goes in v2:
time: 70.8 us; the launch traced here: 70.1 us
  local copies, waits for them, and re-layouts  20.4 us (29%)
  starting transfers between devices  14.9 us (21%)
  Pallas kernels  10.9 us (15%)
  waiting for transfers between devices  9.08 us (13%)
  other arithmetic  7.71 us (11%)
  matrix products  6 us (8%)
  between operations  1.14 us (2%)
    pallas_call x1, Pallas kernels, fourier(): pl.pallas_call(fourier_kernel, out_shape=jax.ShapeDtypeStruct((subgrids,...  10.9 us
    all_to_all x1, waiting for transfers between devices, on_device(): lax.all_to_all(sent, everyone, split_axis=0, concat_axis=0, tiled=True)  6.71 us
    all_to_all x1, starting transfers between devices, on_device(): lax.all_to_all(contrib, 'facet', split_axis=0, concat_axis=1, tiled=True)  6 us
    slice x1, local copies, waits for them, and re-layouts, on_device(): antenna_links[0]  5.02 us
    unnamed x40, local copies, waits for them, and re-layouts  4.73 us
    all_to_all x1, starting transfers between devices, on_device(): lax.all_to_all(outgoing, ('pol', 'tm'), split_axis=0, concat_axis=0, tile...  4.07 us
    all_to_all x1, starting transfers between devices, on_device(): lax.all_to_all(sent, everyone, split_axis=0, concat_axis=0, tiled=True)  4.07 us
    dot_general x5, matrix products, nt_dot(): lax.dot_general(left, right, (((1,), (1,)), ((), ())), preferred_element_...  4.04 us
  transfers between devices with their start and end apart: 5, of which 2 were waited for; matrix products, arithmetic and copies ran while one was open for 33% of the time, Pallas kernels for 16%

profile of v2, /device:TPU:0, one launch (start us, length us, event | category | flops | bytes accessed | tf_op | source)
XLA Modules:
  0.0 70.1 jit_solution(10779976008876751472)
XLA Ops:
  0.6 1.8 %pad_maximum_fusion.8 = bf16[128,1024]{1,0:T(8,128)(2,1)} fusion(bf16[128,512]{1,0:T(8,128)(2,1)} %bitcast.137, bf16[128,512]{1,0:T(8,128)(2,1)} %bitcast.139), kind=kLoop, calls=%fused_computation.49 | loop fusion | flops 524288 | bytes 524288 | tf_op jit(solution)/shard_map/concatenate | solution.py:221
  2.5 0.5 collective-permute-start
  3.0 0.9 %copy-done.1 = f32[64,512]{1,0:T(8,128)S(1)} copy-done((f32[64,512]{1,0:T(8,128)S(1)}, f32[64,512]{1,0:T(8,128)}, u32[]{:S(2)}) %copy-start.1) | copy-done | bytes 131096
  3.9 0.9 %copy-done.2 = f32[64,512]{1,0:T(8,128)S(1)} copy-done((f32[64,512]{1,0:T(8,128)S(1)}, f32[64,512]{1,0:T(8,128)}, u32[]{:S(2)}) %copy-start.2) | copy-done | bytes 131096
  4.8 0.9 %copy-done.3 = f32[64,512]{1,0:T(8,128)S(1)} copy-done((f32[64,512]{1,0:T(8,128)S(1)}, f32[64,512]{1,0:T(8,128)}, u32[]{:S(2)}) %copy-start.3) | copy-done | bytes 131096
  5.7 0.9 %copy-done.4 = f32[64,512]{1,0:T(8,128)S(1)} copy-done((f32[64,512]{1,0:T(8,128)S(1)}, f32[64,512]{1,0:T(8,128)}, u32[]{:S(2)}) %copy-start.4) | copy-done | bytes 131096
  6.6 10.9 %shard_map.275 = bf16[4,2,32,1024]{3,2,1,0:T(8,128)(2,1)} custom-call(f32[64,512]{1,0:T(8,128)S(1)} %copy-done.1, f32[64,512]{1,0:T(8,128)S(1)} %copy-done.2, f32[64,512]{1,0:T(8,128)S(1)} %copy-done.3, f32[64,512]{1,0:T(8,128)S(1)} %copy-done.4, bf16[16,2,32,4096]{3,2,1,0:T(8,128)(2,1)} %bitcast.123), custom_call_target="tpu_custom_call" | custom-call | tf_op jit(solution)/shard_map/pallas_call | solution.py:94
  17.5 6.0 %all-to-all-start = ((bf16[4,2,32,1024]{3,2,1,0:T(8,128)(2,1)}), bf16[4,2,32,1024]{3,2,1,0:T(8,128)(2,1)S(1)}, u32[]{:S(2)}, u32[]{:S(2)}) async-start(bf16[4,2,32,1024]{3,2,1,0:T(8,128)(2,1)} %shard_map.275), calls=%async_computation | async-start | bytes 1048576 | tf_op jit(solution)/shard_map/all_to_all | solution.py:235
  23.5 0.2 collective-permute-start.1
  23.8 0.2 reduce-window.8
  24.2 5.0 %slice_reduce_fusion.1 = (s32[130816]{0:T(1024)}, s32[130816]{0:T(1024)S(1)}) fusion(s32[2,130816]{1,0:T(2,128)} %param.36), kind=kLoop, calls=%fused_computation.44 | loop fusion | bytes 2093056 | tf_op jit(solution)/shard_map/slice | solution.py:280
  29.2 2.1 %gather_fusion.5 = s32[32]{0:T(128)S(1)} fusion(s32[130816]{0:T(1024)} %get-tuple-element.17, s32[1024]{0:T(1024)S(1)} %get-tuple-element.86), kind=kCustom, calls=%fused_computation.clone | custom fusion | bytes 384 | tf_op jit(solution)/shard_map/jit(_take)/gather | solution.py:280
  31.3 0.7 gather_fusion.6
  32.1 0.6 gather_fusion
  32.7 0.4 fusion.1
  33.2 1.1 %constant_dynamic-slice_fusion = (bf16[8,1,32,512]{3,2,0,1:T(8,128)(2,1)S(1)}, bf16[8,1,32,512]{3,2,0,1:T(8,128)(2,1)S(1)}) fusion(bf16[8,2,32,512]{3,2,0,1:T(8,128)(2,1)} %constant.120, s32[]{:T(128)S(6)} %select_n.66, bf16[8,2,32,512]{3,2,0,1:T(8,128)(2,1)} %constant.119), kind=kLoop, calls=%fused_computation.139 | loop fusion | bytes 1048580 | tf_op jit(solution)/shard_map/jit(dynamic_index_in_dim)/dynamic_slice | solution.py:259
  34.4 1.1 %pad_maximum_fusion.3 = bf16[256,1024]{1,0:T(8,128)(2,1)S(1)} fusion(bf16[128,1024]{1,0:T(8,128)(2,1)} %collective-permute-done, bf16[128,512]{1,0:T(8,128)(2,1)S(1)} %bitcast.138, bf16[128,512]{1,0:T(8,128)(2,1)S(1)} %bitcast.140), kind=kLoop, calls=%fused_computation.36 | loop fusion | flops 1572864 | bytes 1048576 | tf_op jit(solution)/shard_map/concatenate | solution.py:231
  35.5 0.2 fusion.6
  35.7 1.0 %fusion.17 = f32[768,1024]{1,0:T(8,128)S(1)} fusion(bf16[512,1024]{1,0:T(8,128)(2,1)S(1)} %copy-done.6, bf16[256,512]{1,0:T(8,128)(2,1)S(1)} %get-tuple-element.49, bf16[256,512]{1,0:T(8,128)(2,1)S(1)} %get-tuple-element.44, bf16[256,512]{1,0:T(8,128)(2,1)S(1)} %get-tuple-element.48), kind=kOutput, calls=%fused_computation.46 | convolution fusion | flops 807665664 | bytes 4980736 | tf_op jit(solution)/shard_map/dot_general | solution.py:246
  36.7 0.2 copy-done.5
  36.9 1.0 %fusion.16 = f32[768,1024]{1,0:T(8,128)S(1)} fusion(bf16[512,1024]{1,0:T(8,128)(2,1)S(1)} %copy-done.5, bf16[256,512]{1,0:T(8,128)(2,1)S(1)} %get-tuple-element.49, bf16[256,512]{1,0:T(8,128)(2,1)S(1)} %get-tuple-element.44, bf16[256,512]{1,0:T(8,128)(2,1)S(1)} %get-tuple-element.48), kind=kOutput, calls=%fused_computation.45 | convolution fusion | flops 807665664 | bytes 4980736 | tf_op jit(solution)/shard_map/dot_general | solution.py:247
  37.9 0.2 fusion.10
  38.1 0.5 fusion.11
  38.7 1.6 %pad_maximum_fusion = bf16[4,256,1024]{2,1,0:T(8,128)(2,1)} fusion(bf16[1,256,1024]{2,1,0:T(8,128)(2,1)S(1)} %get-tuple-element.38, bf16[1,256,1024]{2,1,0:T(8,128)(2,1)S(1)} %get-tuple-element.79, bf16[1,256,1024]{2,1,0:T(8,128)(2,1)S(1)} %get-tuple-element.37, bf16[1,256,1024]{2,1,0:T(8,128)(2,1)S(1)} %get-tuple-element.78), kind=kLoop, calls=%fused_computation.7 | loop fusion | flops 3145728 | bytes 4194304 | tf_op jit(solution)/shard_map/stack | solution.py:248
  40.3 0.4 fusion.50
  40.7 0.4 fusion.51
  41.1 0.8 %slice_subtract_fusion.1 = (f32[256,1,256]{2,0,1:T(8,128)S(1)}, f32[256,1,256]{2,0,1:T(8,128)S(1)}, f32[256,1,256]{2,0,1:T(8,128)S(1)}, f32[256,1,256]{2,0,1:T(8,128)}) fusion(f32[256,3,256]{2,0,1:T(8,128)S(1)} %fusion.51, f32[256,3,256]{2,0,1:T(8,128)S(1)} %fusion.50), kind=kLoop, calls=%fused_computation.48 | loop fusion | flops 131072 | bytes 2621440 | tf_op jit(solution)/shard_map/sub | solution.py:265
  41.9 2.4 %fusion.52 = f32[256,2,2,256]{3,0,2,1:T(8,128)S(1)} fusion(bf16[256,1024,1,1]{1,0,3,2:T(8,128)(2,1)S(1)} %bitcast.127, bf16[2,2,256,1024]{3,2,1,0:T(8,128)(2,1)} %bitcast.124), kind=kOutput, calls=%fused_computation.154 | convolution fusion | flops 536870912 | bytes 3670016 | tf_op jit(solution)/shard_map/dot_general | solution.py:197
  44.3 0.2 add_reduce_fusion
  44.7 0.7 all_to_all.18
  45.4 4.1 %all-to-all-start.1 = ((f32[8,1,64]{2,1,0:T(1,128)}), f32[8,1,64]{2,1,0:T(1,128)S(1)}, u32[]{:S(2)}, u32[]{:S(2)}) async-start(f32[8,1,64]{2,1,0:T(1,128)} %bitcast.35), calls=%async_computation.1 | async-start | bytes 8192 | tf_op jit(solution)/shard_map/all_to_all | solution.py:273
  49.5 0.6 gather_fusion.2
  50.0 0.6 gather_fusion.4
  50.6 0.6 gather_fusion.1
  51.1 0.6 gather_fusion.3
  51.7 2.4 %all-to-all-done.1 = f32[8,1,64]{2,1,0:T(1,128)S(1)} async-done(((f32[8,1,64]{2,1,0:T(1,128)}), f32[8,1,64]{2,1,0:T(1,128)S(1)}, u32[]{:S(2)}, u32[]{:S(2)}) %all-to-all-start.1) | async-done | bytes 2080 | tf_op jit(solution)/shard_map/all_to_all | solution.py:273
  54.1 0.5 broadcast.197
  54.6 0.7 reduce.20
  55.6 0.6 broadcast_in_dim.62
  56.2 4.1 %all-to-all-start.2 = ((f32[32,1,352]{2,1,0:T(1,128)}), f32[32,1,352]{2,1,0:T(1,128)S(1)}, u32[]{:S(2)}, u32[]{:S(2)}) async-start(f32[32,1,352]{2,1,0:T(1,128)} %broadcast_in_dim.62), calls=%async_computation.2 | async-start | bytes 98304 | tf_op jit(solution)/shard_map/all_to_all | solution.py:302
  60.3 0.6 copy.92
  60.9 6.7 %all-to-all-done.2 = f32[32,1,352]{2,1,0:T(1,128)S(1)} async-done(((f32[32,1,352]{2,1,0:T(1,128)}), f32[32,1,352]{2,1,0:T(1,128)S(1)}, u32[]{:S(2)}, u32[]{:S(2)}) %all-to-all-start.2) | async-done | bytes 45088 | tf_op jit(solution)/shard_map/all_to_all | solution.py:302
  67.6 0.1 reduce.3
  67.8 0.1 reshape.432
  67.9 0.1 slice_reduce_fusion.4
  68.6 0.5 fusion
  69.1 0.2 copy.95
  69.3 0.8 %copy.97 = f32[16,1024]{1,0:T(8,128)} copy(f32[16,1024]{0,1:T(8,128)S(1)} %bitcast.128) | data formatting | bytes 131072
  (88 shorter events, 1.6 us)
Async XLA Ops:
  0.6 31.4 %copy-start = (f32[256,4,512]{2,1,0:T(4,128)S(1)}, f32[256,4,512]{2,1,0:T(4,128)}, u32[]{:S(2)}) copy-start(f32[256,4,512]{2,1,0:T(4,128)} %param.37) | copy-start | bytes 6291460
  2.5 31.9 %collective-permute-start = (bf16[128,1024]{1,0:T(8,128)(2,1)}, bf16[128,1024]{1,0:T(8,128)(2,1)}, u32[]{:S(2)}, u32[]{:S(2)}) collective-permute-start(bf16[128,1024]{1,0:T(8,128)(2,1)} %pad_maximum_fusion.8), channel_id=1, source_target_pairs={{0,1},{1,0},{2,3},{3,2},{4,5},{5,4},{6,7},{7,6},{8,9},{9,8},{10,11... | collective-permute-start | bytes 786440 | tf_op jit(solution)/shard_map/ppermute | solution.py:228
  3.0 0.9 %copy-start.1 = (f32[64,512]{1,0:T(8,128)S(1)}, f32[64,512]{1,0:T(8,128)}, u32[]{:S(2)}) copy-start(f32[64,512]{1,0:T(8,128)} %constant.94.clone.p_ref) | copy-start | bytes 393220
  3.9 0.9 %copy-start.2 = (f32[64,512]{1,0:T(8,128)S(1)}, f32[64,512]{1,0:T(8,128)}, u32[]{:S(2)}) copy-start(f32[64,512]{1,0:T(8,128)} %constant.95.clone.q_ref) | copy-start | bytes 393220
  4.8 0.9 %copy-start.3 = (f32[64,512]{1,0:T(8,128)S(1)}, f32[64,512]{1,0:T(8,128)}, u32[]{:S(2)}) copy-start(f32[64,512]{1,0:T(8,128)} %constant.96.clone.c_ref) | copy-start | bytes 393220
  5.7 0.9 %copy-start.4 = (f32[64,512]{1,0:T(8,128)S(1)}, f32[64,512]{1,0:T(8,128)}, u32[]{:S(2)}) copy-start(f32[64,512]{1,0:T(8,128)} %constant.97.clone.s_ref) | copy-start | bytes 393220
  6.6 16.9 %copy-start.14 = (bf16[1,1,2,128]{3,2,1,0:T(2,128)(2,1)S(1)}, bf16[1,1,2,128]{3,2,1,0:T(2,128)(2,1)}, u32[]{:S(2)}) copy-start(bf16[1,1,2,128]{3,2,1,0:T(2,128)(2,1)} %param.33) | copy-start | bytes 1540
  6.6 17.1 %copy-start.13 = (s32[1,1,3,8]{3,1,2,0:T(1,128)S(1)}, s32[1,1,3,8]{3,1,2,0:T(1,128)}, u32[]{:S(2)}) copy-start(s32[1,1,3,8]{3,1,2,0:T(1,128)} %param.35) | copy-start | bytes 292
  17.5 15.7 %copy-start.17 = (s32[4]{0:T(128)S(1)}, s32[4]{0:T(128)}, u32[]{:S(2)}) copy-start(s32[4]{0:T(128)} %constant.121) | copy-start | bytes 52
  17.5 15.7 %copy-start.18 = (s32[4]{0:T(128)S(1)}, s32[4]{0:T(128)}, u32[]{:S(2)}) copy-start(s32[4]{0:T(128)} %constant.122) | copy-start | bytes 52
  17.5 15.7 %copy-start.15 = (s32[4]{0:T(128)S(1)}, s32[4]{0:T(128)}, u32[]{:S(2)}) copy-start(s32[4]{0:T(128)} %constant.123) | copy-start | bytes 52
  17.5 15.7 %copy-start.16 = (s32[4]{0:T(128)S(1)}, s32[4]{0:T(128)}, u32[]{:S(2)}) copy-start(s32[4]{0:T(128)} %constant.124) | copy-start | bytes 52
  17.5 24.4 %all-to-all-start = ((bf16[4,2,32,1024]{3,2,1,0:T(8,128)(2,1)}), bf16[4,2,32,1024]{3,2,1,0:T(8,128)(2,1)S(1)}, u32[]{:S(2)}, u32[]{:S(2)}) async-start(bf16[4,2,32,1024]{3,2,1,0:T(8,128)(2,1)} %shard_map.275), calls=%async_computation | async-start | bytes 1048576 | tf_op jit(solution)/shard_map/all_to_all | solution.py:235
  23.5 21.0 %collective-permute-start.1 = (bf16[2,128]{1,0:T(2,128)(2,1)S(1)}, bf16[2,128]{1,0:T(2,128)(2,1)S(1)}, u32[]{:S(2)}, u32[]{:S(2)}) collective-permute-start(bf16[2,128]{1,0:T(2,128)(2,1)S(1)} %bitcast.154), channel_id=1, source_target_pairs={{0,1},{1,0},{2,3},{3,2},{4,5},{5,4},{6,7},{7,6},{8,9},{9,8},{10,11... | collective-permute-start | bytes 1544 | tf_op jit(solution)/shard_map/ppermute | solution.py:230
  24.1 10.2 %copy-start.10 = (f32[1,8,1,32]{3,2,1,0:T(1,128)S(1)}, f32[1,8,1,32]{3,2,1,0:T(1,128)}, u32[]{:S(2)}) copy-start(f32[1,8,1,32]{3,2,1,0:T(1,128)} %param.34) | copy-start | bytes 3076
  24.1 10.2 %copy-start.8 = (bf16[1,1,128,512]{3,2,1,0:T(8,128)(2,1)S(1)}, bf16[1,1,128,512]{3,2,1,0:T(8,128)(2,1)}, u32[]{:S(2)}) copy-start(bf16[1,1,128,512]{3,2,1,0:T(8,128)(2,1)} %param.32) | copy-start | bytes 393220
  24.1 10.2 %copy-start.9 = (bf16[1,1,128,512]{3,2,1,0:T(8,128)(2,1)S(1)}, bf16[1,1,128,512]{3,2,1,0:T(8,128)(2,1)}, u32[]{:S(2)}) copy-start(bf16[1,1,128,512]{3,2,1,0:T(8,128)(2,1)} %param.31) | copy-start | bytes 393220
  31.3 4.2 %copy-start.11 = (f32[512]{0:T(512)S(1)}, f32[512]{0:T(512)}, u32[]{:S(2)}) copy-start(f32[512]{0:T(512)} %constant.102.clone) | copy-start | bytes 6148
  31.3 4.2 %copy-start.12 = (f32[512]{0:T(512)S(1)}, f32[512]{0:T(512)}, u32[]{:S(2)}) copy-start(f32[512]{0:T(512)} %constant.103.clone) | copy-start | bytes 6148
  34.3 1.4 %copy-start.6 = (bf16[512,1024]{1,0:T(8,128)(2,1)S(1)}, bf16[512,1024]{1,0:T(8,128)(2,1)}, u32[]{:S(2)}) copy-start(bf16[512,1024]{1,0:T(8,128)(2,1)} %constant.100.clone) | copy-start | bytes 3145732
  35.7 1.2 %copy-start.5 = (bf16[512,1024]{1,0:T(8,128)(2,1)S(1)}, bf16[512,1024]{1,0:T(8,128)(2,1)}, u32[]{:S(2)}) copy-start(bf16[512,1024]{1,0:T(8,128)(2,1)} %constant.101.clone) | copy-start | bytes 3145732
  41.9 2.4 %copy-start.7 = (f32[256,1,256]{2,0,1:T(8,128)S(1)}, f32[256,1,256]{2,0,1:T(8,128)}, u32[]{:S(2)}) copy-start(f32[256,1,256]{2,0,1:T(8,128)} %get-tuple-element.42) | copy-start | bytes 786436
  45.4 8.7 %all-to-all-start.1 = ((f32[8,1,64]{2,1,0:T(1,128)}), f32[8,1,64]{2,1,0:T(1,128)S(1)}, u32[]{:S(2)}, u32[]{:S(2)}) async-start(f32[8,1,64]{2,1,0:T(1,128)} %bitcast.35), calls=%async_computation.1 | async-start | bytes 8192 | tf_op jit(solution)/shard_map/all_to_all | solution.py:273
  56.2 11.4 %all-to-all-start.2 = ((f32[32,1,352]{2,1,0:T(1,128)}), f32[32,1,352]{2,1,0:T(1,128)S(1)}, u32[]{:S(2)}, u32[]{:S(2)}) async-start(f32[32,1,352]{2,1,0:T(1,128)} %broadcast_in_dim.62), calls=%async_computation.2 | async-start | bytes 98304 | tf_op jit(solution)/shard_map/all_to_all | solution.py:302

commit v3 on v2

v3 whole, which is shorter than its diff:
```python
import functools
import math

import jax
import jax.numpy as jnp
import numpy as np
from jax import lax
from jax.experimental import pallas as pl
from jax.experimental.pallas import tpu as pltpu
from jax.sharding import PartitionSpec as P

FGRID = 8
FS = 4096
MC = 64
SG = 512
NPOL = 4
NW = 2
NCH = 256
NST = 512
CHUNK = 512

w_chirp = 0.37
grad_scale = 0.1


def unit_angles(left, right, length):
    product = np.outer(np.arange(left), np.arange(right)) % length
    return 2.0 * math.pi * product / length


def fourier_factors(subgrids):
    spread = FS // MC
    alpha = unit_angles(FS // spread, MC, MC)
    p = np.concatenate([np.cos(alpha), -np.sin(alpha)], axis=1) / math.sqrt(FS)
    q = np.concatenate([-np.sin(alpha), -np.cos(alpha)], axis=1) / math.sqrt(FS)
    beta = unit_angles(spread, subgrids * MC, FS).reshape(spread, subgrids, 1, MC)
    beta = np.broadcast_to(beta, (spread, subgrids, 2, MC)).reshape(spread, subgrids * 2 * MC)
    tile = lambda t: np.tile(t, (1, subgrids)).astype(np.float32)
    return (
        tile(p),
        tile(q),
        np.cos(beta).astype(np.float32),
        np.sin(beta).astype(np.float32),
    )


def fourier_kernel(p_ref, q_ref, c_ref, s_ref, x_ref, o_ref, table, total):
    step = pl.program_id(0)
    facets, _, rows, chunk = x_ref.shape
    subgrids = o_ref.shape[0]
    spread = c_ref.shape[0]
    cosine, sine = c_ref[...], s_ref[...]
    for part in range(chunk // spread):
        lead = p_ref[part : part + 1, :]
        other = q_ref[part : part + 1, :]
        table[part * spread : (part + 1) * spread, :] = (lead * cosine + other * sine).astype(
            jnp.bfloat16
        )
    x = x_ref[...].reshape(facets * 2 * rows, chunk)
    product = jnp.dot(x, table[...], preferred_element_type=jnp.float32)

    @pl.when(step == 0)
    def _():
        total[...] = product

    @pl.when(step > 0)
    def _():
        total[...] += product

    @pl.when(step == pl.num_programs(0) - 1)
    def _():
        lane = lax.broadcasted_iota(jnp.int32, (rows, 2 * MC), 1)
        sign = jnp.where(lane < MC, -1.0, 1.0)
        packed = o_ref.shape[3] // (2 * MC)
        for f in range(facets):
            for s in range(subgrids):
                cut = slice(s * 2 * MC, (s + 1) * 2 * MC)
                first = total[2 * f * rows : (2 * f + 1) * rows, cut]
                second = total[(2 * f + 1) * rows : (2 * f + 2) * rows, cut]
                value = first + sign * pltpu.roll(second, MC, 1)
                j = f % packed
                o_ref[s, f // packed, :, j * 2 * MC : (j + 1) * 2 * MC] = value.astype(jnp.bfloat16)


def fourier(x, subgrids):
    facets, _, rows, length = x.shape
    width = subgrids * 2 * MC
    spread = FS // MC
    packed = FGRID if facets % FGRID == 0 else 1
    per_step = CHUNK // spread
    factors = [jnp.asarray(t) for t in fourier_factors(subgrids)]
    return pl.pallas_call(
        fourier_kernel,
        out_shape=jax.ShapeDtypeStruct(
            (subgrids, facets // packed, rows, packed * 2 * MC), jnp.bfloat16
        ),
        grid=(length // CHUNK,),
        in_specs=[
            pl.BlockSpec((per_step, width), lambda g: (g, 0)),
            pl.BlockSpec((per_step, width), lambda g: (g, 0)),
            pl.BlockSpec((spread, width), lambda g: (0, 0)),
            pl.BlockSpec((spread, width), lambda g: (0, 0)),
            pl.BlockSpec((facets, 2, rows, CHUNK), lambda g: (0, 0, 0, g)),
        ],
        out_specs=pl.BlockSpec(
            (subgrids, facets // packed, rows, packed * 2 * MC), lambda g: (0, 0, 0, 0)
        ),
        scratch_shapes=[
            pltpu.VMEM((CHUNK, width), jnp.bfloat16),
            pltpu.VMEM((facets * 2 * rows, width), jnp.float32),
        ],
        compiler_params=pltpu.CompilerParams(
            dimension_semantics=("arbitrary",), vmem_limit_bytes=48 << 20
        ),
    )(*factors, x)


def subgrid_tables():
    angle = unit_angles(SG, SG, SG)
    re = np.cos(angle) / math.sqrt(SG)
    im = np.sin(angle) / math.sqrt(SG)
    blocks = lambda t: t.reshape(SG, FGRID, MC)
    second = np.stack([blocks(re), -blocks(im)], axis=2).reshape(SG, 2 * SG)
    third = np.stack([blocks(im), blocks(re)], axis=2).reshape(SG, 2 * SG)
    return [t.astype(jnp.bfloat16) for t in (re, im, second, third)]


def chirp_line():
    offset = np.arange(SG) - SG // 2
    angle = 2.0 * math.pi * w_chirp * (offset * offset) / float(SG * SG)
    return np.cos(angle).astype(np.float32), np.sin(angle).astype(np.float32)


def decode_slots(block_table, slot_index):
    channels = block_table[0]
    offsets = block_table[1]
    amounts = block_table[2]
    starts = jnp.cumsum(amounts) - amounts
    relative = slot_index[:, None] - starts[None, :]
    member = ((relative >= 0) & (relative < amounts[None, :])).astype(jnp.int32)
    slot_live = jnp.sum(member, axis=-1)
    channel = jnp.sum(member * channels[None, :], axis=-1)
    baseline = jnp.sum(member * (offsets[None, :] + relative), axis=-1)
    return slot_live, channel, baseline, member


def model_terms(pred, observed, first, second, alive):
    residual, lead, trail = [], [], []
    for p in range(NPOL):
        f1, f2 = p // 2, p % 2
        pred_re, pred_im = pred[p]
        first_re, first_im = first[2 * f1], first[2 * f1 + 1]
        second_re, second_im = second[2 * f2], second[2 * f2 + 1]
        both_re = first_re * second_re + first_im * second_im
        both_im = first_im * second_re - first_re * second_im
        resid_re = alive * (observed[2 * p] - (both_re * pred_re - both_im * pred_im))
        resid_im = alive * (observed[2 * p + 1] - (both_re * pred_im + both_im * pred_re))
        cross_re = second_re * pred_re + second_im * pred_im
        cross_im = second_im * pred_re - second_re * pred_im
        along_re = first_re * pred_re - first_im * pred_im
        along_im = first_re * pred_im + first_im * pred_re
        residual += [resid_re, resid_im]
        lead.append(
            (-(resid_re * cross_re - resid_im * cross_im), -(resid_re * cross_im + resid_im * cross_re))
        )
        trail.append(
            (-(resid_re * along_re + resid_im * along_im), -(resid_re * along_im - resid_im * along_re))
        )
    leading = [lead[2 * f][r] + lead[2 * f + 1][r] for f in range(2) for r in range(2)]
    trailing = [trail[f][r] + trail[f + 2][r] for f in range(2) for r in range(2)]
    return residual, leading, trailing


def nt_dot(left, right, **kw):
    return lax.dot_general(
        left, right, (((1,), (1,)), ((), ())), preferred_element_type=jnp.float32, **kw
    )


def chirped_rows(taper, chirp_ref):
    wide = taper.astype(jnp.float32)
    return jnp.concatenate(
        [
            taper,
            (wide * chirp_ref[0:1, :]).astype(jnp.bfloat16),
            (wide * chirp_ref[1:2, :]).astype(jnp.bfloat16),
        ],
        axis=0,
    )


def predict_kernel(
    sizes,
    contrib_ref,
    lead_ref,
    trail_ref,
    depth_ref,
    observed_ref,
    gains_ref,
    idents_ref,
    table_re_ref,
    table_im_ref,
    second_ref,
    third_ref,
    chirp_ref,
    residual_ref,
    grad_ref,
    got,
    lines,
    tapers,
    right,
    left,
    part_out,
    part_in,
    observed_in,
    record_out,
    record_in,
    got_send,
    got_recv,
    taper_send,
    taper_recv,
    observed_send,
    observed_recv,
    part_send,
    part_recv,
    record_send,
    record_recv,
):
    subgrids, pols, owners = sizes
    z, p, t = lax.axis_index("facet"), lax.axis_index("pol"), lax.axis_index("tm")
    slots = lead_ref.shape[0]
    _, groups, rows, width = contrib_ref.shape
    mesh_id = pl.DeviceIdType.MESH

    def remote(src, dst, send, recv, peer):
        return pltpu.make_async_remote_copy(
            src_ref=src,
            dst_ref=dst,
            send_sem=send,
            recv_sem=recv,
            device_id=peer,
            device_id_type=mesh_id,
        )

    across_total = subgrids * owners
    plane_total = pols * owners
    across = z * owners + t
    plane = p * owners + t

    def across_peer(d):
        other = lax.rem(across + d, across_total)
        return other, (other // owners, p, lax.rem(other, owners))

    def plane_peer(d):
        other = lax.rem(plane + d, plane_total)
        return other, (z, other // owners, lax.rem(other, owners))

    barrier = pltpu.get_barrier_semaphore()
    for d in range(1, across_total):
        pl.semaphore_signal(barrier, inc=1, device_id=across_peer(d)[1], device_id_type=mesh_id)
    for d in range(1, pols):
        q = lax.rem(p + d, pols)
        for o in range(owners):
            pl.semaphore_signal(barrier, inc=1, device_id=(z, q, o), device_id_type=mesh_id)
    pl.semaphore_wait(barrier, across_total - 1 + (pols - 1) * owners)

    copies = []
    for d in range(1, subgrids):
        other = lax.rem(z + d, subgrids)
        copies.append(
            remote(contrib_ref.at[other], got.at[z], got_send.at[d], got_recv.at[d], (other, p, t))
        )
    partner = lax.rem(t + 1, owners)
    taper_copies = [
        remote(ref, tapers.at[t, k], taper_send.at[k], taper_recv.at[k], (z, p, partner))
        for k, ref in enumerate((trail_ref, lead_ref))
    ]
    observed_copies = []
    for d in range(1, pols):
        q = lax.rem(p + d, pols)
        observed_copies.append(
            remote(
                observed_ref, observed_in.at[p], observed_send.at[d], observed_recv.at[d], (z, q, t)
            )
        )
    for copy in copies + taper_copies + observed_copies:
        copy.start()

    table_re = jnp.concatenate([table_re_ref[i, t] for i in range(FGRID)], axis=0)
    table_im = jnp.concatenate([table_im_ref[i, t] for i in range(FGRID)], axis=0)

    def prepare(owner, trail, lead):
        trail3 = chirped_rows(trail, chirp_ref)
        a = jnp.dot(trail3, second_ref[...], preferred_element_type=jnp.float32)
        b = jnp.dot(trail3, third_ref[...], preferred_element_type=jnp.float32)
        n0, n1, n2 = slice(0, slots), slice(slots, 2 * slots), slice(2 * slots, 3 * slots)
        right[owner, 0:slots, :] = a[n0].astype(jnp.bfloat16)
        right[owner, slots : 2 * slots, :] = (a[n1] - b[n2]).astype(jnp.bfloat16)
        right[owner, 2 * slots : 3 * slots, :] = b[n0].astype(jnp.bfloat16)
        right[owner, 3 * slots : 4 * slots, :] = (b[n1] + a[n2]).astype(jnp.bfloat16)
        lead3 = chirped_rows(lead, chirp_ref)
        u = nt_dot(table_re, lead3)
        v = nt_dot(table_im, lead3)
        left[owner, 0] = u[:, n0]
        left[owner, 1] = v[:, n0]
        left[owner, 2] = u[:, n1] - v[:, n2]
        left[owner, 3] = u[:, n2] + v[:, n1]

    prepare(t, trail_ref[...], lead_ref[...])
    got[z] = contrib_ref[z]
    for copy in taper_copies:
        copy.wait()
    prepare(partner, tapers[partner, 0], tapers[partner, 1])
    for copy in copies:
        copy.wait()
    if width == 2 * SG:
        whole = got[...].reshape(subgrids * groups * rows, width)
    else:
        for f in range(subgrids * groups):
            i, j = f // FGRID, f % FGRID
            lines[i * rows : (i + 1) * rows, j * 2 * MC : (j + 1) * 2 * MC] = got[
                f // groups, f % groups
            ]
        whole = lines[...]
    for o in range(owners):
        spread = nt_dot(whole, right[o])
        for w in range(NW):
            g_re = spread[:, w * slots : (w + 1) * slots]
            g_im = spread[:, (NW + w) * slots : (NW + w + 1) * slots]
            l_re, l_im = left[o, 2 * w], left[o, 2 * w + 1]
            part_out[o, 2 * w : 2 * w + 1, :] = jnp.sum(l_re * g_re - l_im * g_im, axis=0, keepdims=True)
            part_out[o, 2 * w + 1 : 2 * w + 2, :] = jnp.sum(
                l_re * g_im + l_im * g_re, axis=0, keepdims=True
            )
        part_out[o, 2 * NW :, :] = jnp.zeros((8 - 2 * NW, slots), jnp.float32)

    part_copies = []
    for d in range(1, plane_total):
        other, peer = plane_peer(d)
        part_copies.append(
            remote(
                part_out.at[lax.rem(other, owners)],
                part_in.at[plane],
                part_send.at[d],
                part_recv.at[d],
                peer,
            )
        )
    for copy in part_copies:
        copy.start()
    part_in[plane] = part_out[t]
    observed_in[p] = observed_ref[...]
    for copy in observed_copies:
        copy.wait()
    observed = observed_in[0]
    for q in range(1, pols):
        observed = observed + observed_in[q]
    depth = depth_ref[...].astype(jnp.float32)
    for copy in part_copies:
        copy.wait()

    pred = []
    per_pol = part_in.shape[0] // NPOL
    for q in range(NPOL):
        block = part_in[q * per_pol]
        for o in range(1, per_pol):
            block = block + part_in[q * per_pol + o]
        pred.append(
            tuple(
                sum(depth[w : w + 1] * block[2 * w + c : 2 * w + c + 1] for w in range(NW))
                for c in range(2)
            )
        )
    gains = gains_ref[...]
    idents = idents_ref[...]
    residual, leading, trailing = model_terms(
        pred,
        [observed[k : k + 1] for k in range(2 * NPOL)],
        [gains[k : k + 1] for k in range(4)],
        [gains[4 + k : 5 + k] for k in range(4)],
        idents[3:4],
    )
    for k in range(3):
        record_out[k : k + 1, :] = idents[k : k + 1]
    for k in range(4):
        record_out[3 + k : 4 + k, :] = leading[k]
        record_out[7 + k : 8 + k, :] = trailing[k]
    record_out[11:, :] = jnp.zeros((5, slots), jnp.float32)
    record_copies = []
    for d in range(1, across_total):
        other, peer = across_peer(d)
        record_copies.append(
            remote(record_out, record_in.at[across], record_send.at[d], record_recv.at[d], peer)
        )
    for copy in record_copies:
        copy.start()
    record_in[across] = record_out[...]
    for k in range(2 * NPOL):
        residual_ref[k : k + 1, :] = residual[k]
    for copy in record_copies:
        copy.wait()

    piece = jnp.concatenate([record_in[d] for d in range(across_total)], axis=1)
    own_count = grad_ref.shape[1]
    index = (z * pols + p) * owners + t
    mine = (index * own_count + lax.broadcasted_iota(jnp.int32, (own_count, 1), 0)).astype(
        jnp.float32
    )
    match_first = mine == piece[0:1]
    match_second = mine == piece[1:2]
    weighted = jnp.concatenate(
        [
            jnp.where(match_first, piece[3 + k : 4 + k], 0.0)
            + jnp.where(match_second, piece[7 + k : 8 + k], 0.0)
            for k in range(4)
        ],
        axis=0,
    )
    high = weighted.astype(jnp.bfloat16)
    low = (weighted - high.astype(jnp.float32)).astype(jnp.bfloat16)
    channel_ids = lax.broadcasted_iota(jnp.int32, (NCH, 1), 0).astype(jnp.float32)
    onehot = jnp.where(channel_ids == piece[2:3], 1.0, 0.0).astype(jnp.bfloat16)
    summed = nt_dot(high, onehot) + nt_dot(low, onehot)
    for k in range(4):
        grad_ref[k] = grad_scale * summed[k * own_count : (k + 1) * own_count]


def predict(sizes, own_count, *operands):
    subgrids, pols, owners = sizes
    contrib, lead = operands[0], operands[1]
    _, groups, rows, width = contrib.shape
    slots = lead.shape[0]
    vmem = pl.BlockSpec(memory_space=pltpu.VMEM)
    dma = lambda n: pltpu.SemaphoreType.DMA((n,))
    across_total, plane_total = subgrids * owners, pols * owners
    return pl.pallas_call(
        functools.partial(predict_kernel, sizes),
        out_shape=(
            jax.ShapeDtypeStruct((2 * NPOL, slots), jnp.float32),
            jax.ShapeDtypeStruct((4, own_count, NCH), jnp.float32),
        ),
        in_specs=[vmem] * len(operands),
        out_specs=(vmem, vmem),
        scratch_shapes=[
            pltpu.VMEM(contrib.shape, jnp.bfloat16),
            pltpu.VMEM((FGRID * rows, 2 * SG), jnp.bfloat16),
            pltpu.VMEM((owners, 2, slots, SG), jnp.bfloat16),
            pltpu.VMEM((owners, 2 * NW * slots, 2 * SG), jnp.bfloat16),
            pltpu.VMEM((owners, 4, FGRID * rows, slots), jnp.float32),
            pltpu.VMEM((owners, 8, slots), jnp.float32),
            pltpu.VMEM((plane_total, 8, slots), jnp.float32),
            pltpu.VMEM((pols, 8, slots), jnp.float32),
            pltpu.VMEM((16, slots), jnp.float32),
            pltpu.VMEM((across_total, 16, slots), jnp.float32),
            dma(subgrids),
            dma(subgrids),
            dma(2),
            dma(2),
            dma(pols),
            dma(pols),
            dma(plane_total),
            dma(plane_total),
            dma(across_total),
            dma(across_total),
        ],
        compiler_params=pltpu.CompilerParams(
            collective_id=0, has_side_effects=True, vmem_limit_bytes=48 << 20
        ),
    )(*operands)


def on_device(
    tile_spectral_lines,
    taper_leading_axis,
    taper_trailing_axis,
    depth_layer_factors,
    measured_correlations,
    visibility_groups_table,
    antenna_links,
    complex_receiver_factors,
):
    exact = lax.Precision.HIGHEST
    sizes = tuple(lax.axis_size(name) for name in ("facet", "pol", "tm"))
    subgrids, pols, owners = sizes
    slots = taper_leading_axis.shape[2]
    quarter = measured_correlations.shape[3]
    rows = tile_spectral_lines.shape[3]
    pol_index = lax.axis_index("pol")

    slot_index = jnp.arange(slots, dtype=jnp.int32)
    block_table = visibility_groups_table.reshape(3, visibility_groups_table.shape[3])
    slot_live, channel, baseline, member = decode_slots(block_table, slot_index)
    stations = jnp.stack(
        [jnp.take(antenna_links[0], baseline), jnp.take(antenna_links[1], baseline)]
    )
    channel_gains = jnp.take(complex_receiver_factors, block_table[0], axis=0)
    blocks = block_table.shape[1]
    pick = (
        stations.reshape(2 * slots)[:, None] == jnp.arange(NST, dtype=jnp.int32)[None, :]
    ).astype(jnp.float32)
    gains = nt_dot(channel_gains.reshape(blocks * 4, NST), pick, precision=exact)
    gains = gains.reshape(blocks, 4, 2, slots)
    weight = jnp.transpose(member).astype(jnp.float32)[:, None, None, :]
    gains = jnp.sum(gains * weight, axis=0)
    gains = jnp.transpose(gains, (1, 0, 2)).reshape(8, slots)
    idents = jnp.concatenate(
        [stations, channel[None], slot_live[None], jnp.zeros((4, slots), jnp.int32)], axis=0
    ).astype(jnp.float32)

    observed = measured_correlations.reshape(2 * NPOL, quarter)
    in_quarter = (jnp.arange(slots, dtype=jnp.int32) // quarter == pol_index)[None, :]
    observed = jnp.where(in_quarter, jnp.tile(observed, (1, pols)), 0.0)

    contrib = fourier(tile_spectral_lines[:, 0], subgrids)
    table_re, table_im, second, third = [jnp.asarray(t) for t in subgrid_tables()]
    cosine, sine = chirp_line()
    own_count = NST // (subgrids * pols * owners)
    residual, grad = predict(
        sizes,
        own_count,
        contrib,
        taper_leading_axis.reshape(slots, SG),
        taper_trailing_axis.reshape(slots, SG),
        depth_layer_factors.reshape(NW, slots),
        observed,
        gains,
        idents,
        table_re.reshape(FGRID, owners, rows, SG),
        table_im.reshape(FGRID, owners, rows, SG),
        second,
        third,
        jnp.asarray(np.stack([cosine, sine])),
    )
    residual = lax.dynamic_slice_in_dim(residual, pol_index * quarter, quarter, 1)
    gain_grad = jnp.transpose(grad, (1, 2, 0)).reshape(own_count, 4 * NCH)
    return residual.reshape(1, 2 * NPOL, 1, quarter), gain_grad


def solution(mesh):
    return jax.shard_map(
        on_device,
        mesh=mesh,
        in_specs=(
            P("facet", "pol", None, "tm", None),
            P("facet", "tm", None, None),
            P("facet", "tm", None, None),
            P("facet", "tm", None, None),
            P("facet", None, "tm", "pol"),
            P("facet", "tm", None, None),
            P(),
            P(),
        ),
        out_specs=(P("facet", None, "tm", "pol"), P(("facet", "pol", "tm"), None)),
        check_vma=False,
    )
```

time: 70.8 us -> 55.4 us (0.78)
  Pallas kernels: 10.9 us -> 39.6 us
  starting transfers between devices: 14.9 us -> 0 us
  waiting for transfers between devices: 9.08 us -> 0 us
  local copies, waits for them, and re-layouts: 20.4 us -> 12.5 us
  other arithmetic: 7.71 us -> 1.15 us
  matrix products: 6 us -> 0.44 us
    pallas_call x0 -> x1, Pallas kernels: none -> 29.4 us  [predict(): pl.pallas_call(functools.partial(predict_kernel, sizes), out_shape=(jax.S...]
    all_to_all x3 -> x0, starting transfers between devices: 14.1 us -> none  [the longest x1 6 us: on_device(): lax.all_to_all(contrib, 'facet', split_axis=0, concat_axis=1, tiled=True)]
    all_to_all x3 -> x0, waiting for transfers between devices: 9.07 us -> none  [the longest x1 6.71 us: on_device(): lax.all_to_all(sent, everyone, split_axis=0, concat_axis=0, tiled=True)]
    unnamed x40 -> x31, local copies, waits for them, and re-layouts: 4.73 us -> 0.9 us
    dot_general x5 -> x1, matrix products: 4.04 us -> 0.44 us  [nt_dot(): lax.dot_general(left, right, (((1,), (1,)), ((), ())), preferred_element_...]
    concatenate x3 -> x0, other arithmetic: 2.95 us -> none  [the longest x1 1.83 us: on_device(): jnp.concatenate([taper_leading_axis.reshape(slots, SG), taper_trailing_ax...]
    gather x4 -> x0, local copies, waits for them, and re-layouts: 2.23 us -> none  [the longest x1 0.56 us: model_terms(): second_re = gain_second[2 * feed_second]]
    dot_general x2 -> x0, matrix products: 1.96 us -> none  [the longest x1 0.98 us: on_device(): jnp.dot(trail3, third, preferred_element_type=jnp.float32)]
  transfers between devices with their start and end apart: 5 -> 0, of which waited for: 2 -> 0; matrix products, arithmetic and copies ran while one was open for 33% -> 0% of each run, Pallas kernels for 16% -> 0%
where the time goes in v3:
time: 55.4 us; the launch traced here: 54.7 us
  Pallas kernels  39.6 us (71%)
  local copies, waits for them, and re-layouts  12.5 us (23%)
  other arithmetic  1.15 us (2%)
  between operations  0.97 us (2%)
    pallas_call x1, Pallas kernels, predict(): pl.pallas_call(functools.partial(predict_kernel, sizes), out_shape=(jax.S...  29.4 us
    pallas_call x1, Pallas kernels, fourier(): pl.pallas_call(fourier_kernel, out_shape=jax.ShapeDtypeStruct((subgrids,...  10.2 us
    slice x1, local copies, waits for them, and re-layouts, on_device(): antenna_links[0]  5.01 us
    gather x1, local copies, waits for them, and re-layouts, on_device(): jnp.take(antenna_links[0], baseline)  3 us
    gather x1, local copies, waits for them, and re-layouts, on_device(): jnp.take(antenna_links[1], baseline)  1.15 us

profile of v3, /device:TPU:0, one launch (start us, length us, event | category | flops | bytes accessed | tf_op | source)
XLA Modules:
  0.0 54.7 jit_solution(5250405220104892145)
XLA Ops:
  0.6 0.0 copy-start
  0.6 0.0 copy-start.5
  0.7 0.0 copy-start.6
  0.7 0.0 copy-start.7
  0.7 0.0 copy-start.8
  0.7 0.0 copy-start.14
  0.7 0.0 copy-start.13
  0.7 0.8 %slice_bitcast_fusion = (s32[8]{0:T(128)S(1)}, s32[8]{0:T(128)S(1)}, s32[8]{0:T(128)S(1)}, s32[8,1]{0,1:T(1,128)S(1)}) fusion(s32[1,1,3,8]{3,1,2,0:T(1,128)} %param.24), kind=kLoop, calls=%fused_computation.42 | loop fusion | bytes 224 | tf_op jit(solution)/shard_map/add | solution.py:143
  1.5 0.2 reduce-window.8
  1.7 0.7 %bitcast_subtract_fusion = s32[8]{0:T(128)S(1)} fusion(s32[8,1]{0,1:T(1,128)S(1)} %reduce-window.8, s32[1,1,3,8]{3,1,2,0:T(1,128)} %param.24), kind=kLoop, calls=%fused_computation.39 | loop fusion | flops 8 | bytes 96 | tf_op jit(solution)/shard_map/sub | solution.py:138
  2.4 0.1 convert_reduce_fusion
  2.5 5.0 %slice_reduce_fusion.1 = (s32[130816]{0:T(1024)}, s32[130816]{0:T(1024)S(1)}) fusion(s32[2,130816]{1,0:T(2,128)} %param.25), kind=kLoop, calls=%fused_computation.8 | loop fusion | bytes 2093056 | tf_op jit(solution)/shard_map/slice | solution.py:494
  7.5 3.0 %gather_fusion.1 = s32[128]{0:T(128)S(1)} fusion(s32[130816]{0:T(1024)} %get-tuple-element.13, s32[1024]{0:T(1024)S(1)} %pad_clamp_fusion), kind=kCustom, calls=%fused_computation.clone | custom fusion | bytes 1536 | tf_op jit(solution)/shard_map/jit(_take)/gather | solution.py:494
  10.5 1.1 %gather_fusion.2 = s32[128]{0:T(128)S(1)} fusion(s32[130816]{0:T(1024)S(1)} %get-tuple-element.14, s32[1024]{0:T(1024)S(1)} %pad_clamp_fusion), kind=kCustom, calls=%fused_computation.1.clone | custom fusion | bytes 1536 | tf_op jit(solution)/shard_map/jit(_take)/gather | solution.py:494
  11.7 0.1 convert_convert_fusion
  11.8 0.0 copy-done.14
  11.8 0.0 copy-done
  11.9 0.6 %gather_fusion = f32[8,4,512]{2,1,0:T(4,128)S(1)} fusion(f32[256,4,512]{2,1,0:T(4,128)S(1)} %copy-done, s32[1024]{0:T(1024)S(1)} %pad_clamp_fusion.1), kind=kCustom, calls=%fused_computation.2 | custom fusion | bytes 131104 | tf_op jit(solution)/shard_map/jit(_take)/gather | solution.py:496
  12.5 0.1 select_bitcast_fusion
  12.5 0.4 fusion
  13.0 0.0 copy-done.13
  13.0 0.1 tile.12
  13.1 0.0 copy-done.5
  13.1 0.0 copy-done.6
  13.1 0.0 copy-done.7
  13.1 0.0 copy-done.8
  13.1 0.0 copy-start.1
  13.2 0.0 copy-start.2
  13.2 0.0 copy-start.3
  13.2 0.0 copy-start.4
  13.2 0.0 copy-start.9
  13.2 0.0 copy-start.10
  13.2 0.0 copy-start.11
  13.2 0.0 copy-start.12
  13.2 10.2 %shard_map.176.contrib_ref = bf16[4,2,32,1024]{3,2,1,0:T(8,128)(2,1)S(1)} custom-call(f32[64,512]{1,0:T(8,128)S(1)} %copy-done.5, f32[64,512]{1,0:T(8,128)S(1)} %copy-done.6, f32[64,512]{1,0:T(8,128)S(1)} %copy-done.7, f32[64,512]{1,0:T(8,128)S(1)} %copy-done.8, bf16[16,2,32,4096]{3,2,1,0:T(8,128)(2,1)} %bitcast.44), custom_call_target="tpu_custom_call" | custom-call | tf_op jit(solution)/shard_map/pallas_call | solution.py:92
  23.5 0.0 copy-done.1
  23.5 0.0 copy-done.2
  23.5 0.0 copy-done.3
  23.5 0.0 copy-done.4
  23.5 0.0 copy-done.9
  23.5 0.0 copy-done.10
  23.6 0.0 copy-done.11
  23.6 0.0 copy-done.12
  23.6 29.4 %shard_map.177 = (f32[8,128]{1,0:T(8,128)S(1)}, f32[4,16,256]{2,1,0:T(8,128)S(1)}) custom-call(bf16[4,2,32,1024]{3,2,1,0:T(8,128)(2,1)S(1)} %shard_map.176.contrib_ref, bf16[128,512]{1,0:T(8,128)(2,1)S(1)} %bitcast.39, bf16[128,512]{1,0:T(8,128)(2,1)S(1)} %bitcast.40, bf16[2,128]{1,0:T(2,128)(2,1)S(1)} %bitcast.43, ...), custom_call_target="tpu_custom_call" | custom-call | tf_op jit(solution)/shard_map/pallas_call | solution.py:436
  53.0 0.2 copy.29
  53.2 0.8 %copy.30 = f32[16,1024]{1,0:T(8,128)} copy(f32[16,1024]{0,1:T(8,128)S(1)} %bitcast.45) | data formatting | bytes 131072
  54.0 0.7 %constant_dynamic-slice_fusion = f32[8,32]{1,0:T(8,128)} fusion(f32[8,128]{1,0:T(8,128)S(1)} %get-tuple-element.5, s32[]{:T(128)S(6)} %select_n.53), kind=kLoop, calls=%fused_computation.46 | loop fusion | bytes 2052 | tf_op jit(solution)/shard_map/dynamic_slice | solution.py:534
  (14 shorter events, 0.1 us)
Async XLA Ops:
  0.6 11.2 %copy-start = (f32[256,4,512]{2,1,0:T(4,128)S(1)}, f32[256,4,512]{2,1,0:T(4,128)}, u32[]{:S(2)}) copy-start(f32[256,4,512]{2,1,0:T(4,128)} %param.26) | copy-start | bytes 6291460
  0.6 12.5 %copy-start.5 = (f32[64,512]{1,0:T(8,128)S(1)}, f32[64,512]{1,0:T(8,128)}, u32[]{:S(2)}) copy-start(f32[64,512]{1,0:T(8,128)} %constant.80.clone.p_ref) | copy-start | bytes 393220
  0.7 12.5 %copy-start.6 = (f32[64,512]{1,0:T(8,128)S(1)}, f32[64,512]{1,0:T(8,128)}, u32[]{:S(2)}) copy-start(f32[64,512]{1,0:T(8,128)} %constant.81.clone.q_ref) | copy-start | bytes 393220
  0.7 12.5 %copy-start.7 = (f32[64,512]{1,0:T(8,128)S(1)}, f32[64,512]{1,0:T(8,128)}, u32[]{:S(2)}) copy-start(f32[64,512]{1,0:T(8,128)} %constant.82.clone.c_ref) | copy-start | bytes 393220
  0.7 12.5 %copy-start.8 = (f32[64,512]{1,0:T(8,128)S(1)}, f32[64,512]{1,0:T(8,128)}, u32[]{:S(2)}) copy-start(f32[64,512]{1,0:T(8,128)} %constant.83.clone.s_ref) | copy-start | bytes 393220
  0.7 11.1 %copy-start.14 = (s32[1,1,3,8]{3,1,2,0:T(1,128)S(1)}, s32[1,1,3,8]{3,1,2,0:T(1,128)}, u32[]{:S(2)}) copy-start(s32[1,1,3,8]{3,1,2,0:T(1,128)} %param.24) | copy-start | bytes 292
  0.7 12.3 %copy-start.13 = (f32[1,8,1,32]{3,2,1,0:T(1,128)S(1)}, f32[1,8,1,32]{3,2,1,0:T(1,128)}, u32[]{:S(2)}) copy-start(f32[1,8,1,32]{3,2,1,0:T(1,128)} %param.23) | copy-start | bytes 3076
  13.1 10.3 %copy-start.1 = (bf16[512,1024]{1,0:T(8,128)(2,1)S(1)}, bf16[512,1024]{1,0:T(8,128)(2,1)}, u32[]{:S(2)}) copy-start(bf16[512,1024]{1,0:T(8,128)(2,1)} %constant.86.clone.second_ref) | copy-start | bytes 3145732
  13.2 10.3 %copy-start.2 = (bf16[512,1024]{1,0:T(8,128)(2,1)S(1)}, bf16[512,1024]{1,0:T(8,128)(2,1)}, u32[]{:S(2)}) copy-start(bf16[512,1024]{1,0:T(8,128)(2,1)} %constant.87.clone.third_ref) | copy-start | bytes 3145732
  13.2 10.3 %copy-start.3 = (bf16[8,2,32,512]{3,2,1,0:T(8,128)(2,1)S(1)}, bf16[8,2,32,512]{3,2,1,0:T(8,128)(2,1)}, u32[]{:S(2)}) copy-start(bf16[8,2,32,512]{3,2,1,0:T(8,128)(2,1)} %constant.95.table_re_ref) | copy-start | bytes 1572868
  13.2 10.3 %copy-start.4 = (bf16[8,2,32,512]{3,2,1,0:T(8,128)(2,1)S(1)}, bf16[8,2,32,512]{3,2,1,0:T(8,128)(2,1)}, u32[]{:S(2)}) copy-start(bf16[8,2,32,512]{3,2,1,0:T(8,128)(2,1)} %constant.96.table_im_ref) | copy-start | bytes 1572868
  13.2 10.3 %copy-start.9 = (bf16[1,1,128,512]{3,2,1,0:T(8,128)(2,1)S(1)}, bf16[1,1,128,512]{3,2,1,0:T(8,128)(2,1)}, u32[]{:S(2)}) copy-start(bf16[1,1,128,512]{3,2,1,0:T(8,128)(2,1)} %param.20) | copy-start | bytes 393220
  13.2 10.3 %copy-start.10 = (bf16[1,1,128,512]{3,2,1,0:T(8,128)(2,1)S(1)}, bf16[1,1,128,512]{3,2,1,0:T(8,128)(2,1)}, u32[]{:S(2)}) copy-start(bf16[1,1,128,512]{3,2,1,0:T(8,128)(2,1)} %param.21) | copy-start | bytes 393220
  13.2 10.3 %copy-start.11 = (f32[2,512]{1,0:T(2,128)S(1)}, f32[2,512]{1,0:T(2,128)}, u32[]{:S(2)}) copy-start(f32[2,512]{1,0:T(2,128)} %constant.88.clone.chirp_ref) | copy-start | bytes 12292
  13.2 10.3 %copy-start.12 = (bf16[1,1,2,128]{3,2,1,0:T(2,128)(2,1)S(1)}, bf16[1,1,2,128]{3,2,1,0:T(2,128)(2,1)}, u32[]{:S(2)}) copy-start(bf16[1,1,2,128]{3,2,1,0:T(2,128)(2,1)} %param.22) | copy-start | bytes 1540

commit v4 on v3

--- a/solution.py
+++ b/solution.py
@@ -44,8 +44,111 @@
     )
 
 
-def fourier_kernel(p_ref, q_ref, c_ref, s_ref, x_ref, o_ref, table, total):
+def fetch_lookups(block_ref, links_ref, gain_ref, window, channel_gain, window_sem, gain_sem):
+    blocks, _, span = window.shape
+    copies = []
+    for b in range(blocks):
+        first = jnp.minimum(block_ref[1, b] // 128 * 128, links_ref.shape[1] - span)
+        first = pl.multiple_of(first, 128)
+        copies.append(
+            pltpu.make_async_copy(
+                links_ref.at[:, pl.ds(first, span)], window.at[b], window_sem.at[b]
+            )
+        )
+        copies.append(
+            pltpu.make_async_copy(
+                gain_ref.at[block_ref[0, b]], channel_gain.at[b], gain_sem.at[b]
+            )
+        )
+    return copies
+
+
+def use_lookups(block_ref, links_ref, window, channel_gain, gains_ref, idents_ref):
+    blocks, _, span = window.shape
+    slots = idents_ref.shape[1]
+    lane = lax.broadcasted_iota(jnp.int32, (1, slots), 1)
+    place = lax.broadcasted_iota(jnp.int32, (span, slots), 0)
+    lane_tall = lax.broadcasted_iota(jnp.int32, (span, slots), 1)
+    begin = jnp.int32(0)
+    member, picks = [], []
+    channel = jnp.zeros((1, slots), jnp.float32)
+    alive = jnp.zeros((1, slots), jnp.float32)
+    for b in range(blocks):
+        offset, amount = block_ref[1, b], block_ref[2, b]
+        first = jnp.minimum(offset // 128 * 128, links_ref.shape[1] - span)
+        inside = jnp.where((lane >= begin) & (lane < begin + amount), 1.0, 0.0)
+        member.append(inside)
+        alive += inside
+        channel += inside * block_ref[0, b].astype(jnp.float32)
+        hit = place == lane_tall + (offset - first - begin)
+        picks.append((jnp.where(hit, 1.0, 0.0) * inside).astype(jnp.bfloat16))
+        begin = begin + amount
+    links = jnp.concatenate([window[b] for b in range(blocks)], axis=1)
+    upper = links // 16
+    lower = links - 16 * upper
+    pieces = jnp.concatenate([upper, lower], axis=0).astype(jnp.float32).astype(jnp.bfloat16)
+    found = jnp.dot(
+        pieces, jnp.concatenate(picks, axis=0), preferred_element_type=jnp.float32
+    )
+    stations = 16.0 * found[0:2] + found[2:4]
+    table = channel_gain[...].reshape(blocks * 4, channel_gain.shape[2])
+    high = table.astype(jnp.bfloat16)
+    rest = table - high.astype(jnp.float32)
+    middle = rest.astype(jnp.bfloat16)
+    low = (rest - middle.astype(jnp.float32)).astype(jnp.bfloat16)
+    names = lax.broadcasted_iota(jnp.int32, (table.shape[1], 1), 0).astype(jnp.float32)
+    for side in range(2):
+        pick = jnp.where(names == stations[side : side + 1], 1.0, 0.0).astype(jnp.bfloat16)
+        rows = (
+            jnp.dot(high, pick, preferred_element_type=jnp.float32)
+            + jnp.dot(middle, pick, preferred_element_type=jnp.float32)
+            + jnp.dot(low, pick, preferred_element_type=jnp.float32)
+        )
+        chosen = member[0] * rows[0:4]
+        for b in range(1, blocks):
+            chosen = chosen + member[b] * rows[4 * b : 4 * b + 4]
+        gains_ref[4 * side : 4 * side + 4, :] = chosen
+    idents_ref[0:2, :] = stations
+    idents_ref[2:3, :] = channel
+    idents_ref[3:4, :] = alive
+    idents_ref[4:8, :] = jnp.zeros((4, slots), jnp.float32)
+
+
+def fourier_kernel(
+    block_ref,
+    links_ref,
+    gain_ref,
+    p_ref,
+    q_ref,
+    c_ref,
+    s_ref,
+    x_ref,
+    o_ref,
+    gains_ref,
+    idents_ref,
+    table,
+    total,
+    window,
+    channel_gain,
+    window_sem,
+    gain_sem,
+):
     step = pl.program_id(0)
+    copies = fetch_lookups(
+        block_ref, links_ref, gain_ref, window, channel_gain, window_sem, gain_sem
+    )
+
+    @pl.when(step == 0)
+    def _():
+        for copy in copies:
+            copy.start()
+
+    @pl.when(step == pl.num_programs(0) - 1)
+    def _():
+        for copy in copies:
+            copy.wait()
+        use_lookups(block_ref, links_ref, window, channel_gain, gains_ref, idents_ref)
+
     facets, _, rows, chunk = x_ref.shape
     subgrids = o_ref.shape[0]
     spread = c_ref.shape[0]
@@ -82,37 +185,58 @@
                 o_ref[s, f // packed, :, j * 2 * MC : (j + 1) * 2 * MC] = value.astype(jnp.bfloat16)
 
 
-def fourier(x, subgrids):
+def fourier(x, subgrids, slots, block_table, links, station_gains):
     facets, _, rows, length = x.shape
     width = subgrids * 2 * MC
     spread = FS // MC
     packed = FGRID if facets % FGRID == 0 else 1
     per_step = CHUNK // spread
-    factors = [jnp.asarray(t) for t in fourier_factors(subgrids)]
+    blocks = block_table.shape[1]
+    span = slots + 128
+    in_place = lambda array: pltpu.with_memory_space_constraint(array, pltpu.HBM)
+    factors = [in_place(jnp.asarray(t)) for t in fourier_factors(subgrids)]
+    out = (subgrids, facets // packed, rows, packed * 2 * MC)
     return pl.pallas_call(
         fourier_kernel,
-        out_shape=jax.ShapeDtypeStruct(
-            (subgrids, facets // packed, rows, packed * 2 * MC), jnp.bfloat16
+        out_shape=(
+            jax.ShapeDtypeStruct(out, jnp.bfloat16),
+            jax.ShapeDtypeStruct((8, slots), jnp.float32),
+            jax.ShapeDtypeStruct((8, slots), jnp.float32),
         ),
         grid=(length // CHUNK,),
         in_specs=[
+            pl.BlockSpec(memory_space=pltpu.SMEM),
+            pl.BlockSpec(memory_space=pltpu.HBM),
+            pl.BlockSpec(memory_space=pltpu.HBM),
             pl.BlockSpec((per_step, width), lambda g: (g, 0)),
             pl.BlockSpec((per_step, width), lambda g: (g, 0)),
             pl.BlockSpec((spread, width), lambda g: (0, 0)),
             pl.BlockSpec((spread, width), lambda g: (0, 0)),
             pl.BlockSpec((facets, 2, rows, CHUNK), lambda g: (0, 0, 0, g)),
         ],
-        out_specs=pl.BlockSpec(
-            (subgrids, facets // packed, rows, packed * 2 * MC), lambda g: (0, 0, 0, 0)
+        out_specs=(
+            pl.BlockSpec(out, lambda g: (0, 0, 0, 0)),
+            pl.BlockSpec((8, slots), lambda g: (0, 0)),
+            pl.BlockSpec((8, slots), lambda g: (0, 0)),
         ),
         scratch_shapes=[
             pltpu.VMEM((CHUNK, width), jnp.bfloat16),
             pltpu.VMEM((facets * 2 * rows, width), jnp.float32),
+            pltpu.VMEM((blocks, 2, span), jnp.int32),
+            pltpu.VMEM((blocks, 4, NST), jnp.float32),
+            pltpu.SemaphoreType.DMA((blocks,)),
+            pltpu.SemaphoreType.DMA((blocks,)),
         ],
         compiler_params=pltpu.CompilerParams(
             dimension_semantics=("arbitrary",), vmem_limit_bytes=48 << 20
         ),
-    )(*factors, x)
+    )(
+        block_table,
+        in_place(links),
+        in_place(station_gains),
+        *factors,
+        x,
+    )
 
 
 def subgrid_tables():
@@ -129,19 +253,6 @@
     offset = np.arange(SG) - SG // 2
     angle = 2.0 * math.pi * w_chirp * (offset * offset) / float(SG * SG)
     return np.cos(angle).astype(np.float32), np.sin(angle).astype(np.float32)
-
-
-def decode_slots(block_table, slot_index):
-    channels = block_table[0]
-    offsets = block_table[1]
-    amounts = block_table[2]
-    starts = jnp.cumsum(amounts) - amounts
-    relative = slot_index[:, None] - starts[None, :]
-    member = ((relative >= 0) & (relative < amounts[None, :])).astype(jnp.int32)
-    slot_live = jnp.sum(member, axis=-1)
-    channel = jnp.sum(member * channels[None, :], axis=-1)
-    baseline = jnp.sum(member * (offsets[None, :] + relative), axis=-1)
-    return slot_live, channel, baseline, member
 
 
 def model_terms(pred, observed, first, second, alive):
@@ -479,7 +590,6 @@
     antenna_links,
     complex_receiver_factors,
 ):
-    exact = lax.Precision.HIGHEST
     sizes = tuple(lax.axis_size(name) for name in ("facet", "pol", "tm"))
     subgrids, pols, owners = sizes
     slots = taper_leading_axis.shape[2]
@@ -487,31 +597,19 @@
     rows = tile_spectral_lines.shape[3]
     pol_index = lax.axis_index("pol")
 
-    slot_index = jnp.arange(slots, dtype=jnp.int32)
     block_table = visibility_groups_table.reshape(3, visibility_groups_table.shape[3])
-    slot_live, channel, baseline, member = decode_slots(block_table, slot_index)
-    stations = jnp.stack(
-        [jnp.take(antenna_links[0], baseline), jnp.take(antenna_links[1], baseline)]
-    )
-    channel_gains = jnp.take(complex_receiver_factors, block_table[0], axis=0)
-    blocks = block_table.shape[1]
-    pick = (
-        stations.reshape(2 * slots)[:, None] == jnp.arange(NST, dtype=jnp.int32)[None, :]
-    ).astype(jnp.float32)
-    gains = nt_dot(channel_gains.reshape(blocks * 4, NST), pick, precision=exact)
-    gains = gains.reshape(blocks, 4, 2, slots)
-    weight = jnp.transpose(member).astype(jnp.float32)[:, None, None, :]
-    gains = jnp.sum(gains * weight, axis=0)
-    gains = jnp.transpose(gains, (1, 0, 2)).reshape(8, slots)
-    idents = jnp.concatenate(
-        [stations, channel[None], slot_live[None], jnp.zeros((4, slots), jnp.int32)], axis=0
-    ).astype(jnp.float32)
-
     observed = measured_correlations.reshape(2 * NPOL, quarter)
     in_quarter = (jnp.arange(slots, dtype=jnp.int32) // quarter == pol_index)[None, :]
     observed = jnp.where(in_quarter, jnp.tile(observed, (1, pols)), 0.0)
 
-    contrib = fourier(tile_spectral_lines[:, 0], subgrids)
+    contrib, gains, idents = fourier(
+        tile_spectral_lines[:, 0],
+        subgrids,
+        slots,
+        block_table,
+        antenna_links,
+        complex_receiver_factors,
+    )
     table_re, table_im, second, third = [jnp.asarray(t) for t in subgrid_tables()]
     cosine, sine = chirp_line()
     own_count = NST // (subgrids * pols * owners)

time: 55.4 us -> 43.9 us (0.79)
  local copies, waits for them, and re-layouts: 12.5 us -> 3.47 us
  other arithmetic: 1.15 us -> 0.01 us
    slice x1 -> x0, local copies, waits for them, and re-layouts: 5.01 us -> none  [on_device(): antenna_links[0]]
    gather x3 -> x0, local copies, waits for them, and re-layouts: 4.74 us -> none  [the longest x1 3 us: on_device(): jnp.take(antenna_links[0], baseline)]
    pallas_call x1, Pallas kernels: 29.4 us -> 27.9 us  [predict(): pl.pallas_call(functools.partial(predict_kernel, sizes), out_shape=(jax.S...]
    pallas_call x1, Pallas kernels: 10.2 us -> 11.4 us  [fourier(): pl.pallas_call(fourier_kernel, out_shape=(jax.ShapeDtypeStruct(out, jnp.b...]
    add x1 -> x0, local copies, waits for them, and re-layouts: 0.83 us -> none  [decode_slots(): baseline = jnp.sum(member * (offsets[None, :] + relative), axis=-1)]
    another operation x2, local copies, waits for them, and re-layouts: 0.08 us -> 0.89 us  [on_device(): observed = jnp.where(in_quarter, jnp.tile(observed, (1, pols)), 0.0)]
    unnamed x31 -> x18, local copies, waits for them, and re-layouts: 0.9 us -> 1.68 us
    sub x1 -> x0, other arithmetic: 0.66 us -> none  [decode_slots(): starts = jnp.cumsum(amounts) - amounts]
where the time goes in v4:
time: 43.9 us; the launch traced here: 43.6 us
  Pallas kernels  39.3 us (90%)
  local copies, waits for them, and re-layouts  3.47 us (8%)
  between operations  0.79 us (2%)
    pallas_call x1, Pallas kernels, predict(): pl.pallas_call(functools.partial(predict_kernel, sizes), out_shape=(jax.S...  27.9 us
    pallas_call x1, Pallas kernels, fourier(): pl.pallas_call(fourier_kernel, out_shape=(jax.ShapeDtypeStruct(out, jnp.b...  11.4 us
    unnamed x18, local copies, waits for them, and re-layouts  1.68 us
    another operation x2, local copies, waits for them, and re-layouts, on_device(): observed = jnp.where(in_quarter, jnp.tile(observed, (1, pols)), 0.0)  0.89 us

profile of v4, /device:TPU:0, one launch (start us, length us, event | category | flops | bytes accessed | tf_op | source)
XLA Modules:
  0.0 43.6 jit_solution(17584441843791773862)
XLA Ops:
  0.6 0.0 copy-start.2
  0.6 0.0 copy-start.3
  0.7 0.0 copy-start.6
  0.7 0.0 copy-start
  0.7 0.0 copy-start.1
  0.7 0.0 copy-start.7
  0.7 0.0 copy-start.5
  0.7 0.0 copy-start.4
  0.7 0.8 %copy.23 = s32[1,1,3,8]{3,2,1,0:T(4,128)S(1)} copy(s32[1,1,3,8]{3,1,2,0:T(1,128)} %param.22) | data formatting | bytes 192
  1.6 0.8 %tile.11 = f32[8,4,32]{2,1,0:T(4,128)S(1)} broadcast(f32[8,32]{1,0:T(8,128)} %bitcast.18), dimensions={0,2} | broadcast | bytes 5120 | tf_op jit(solution)/shard_map/tile | solution.py:603
  2.4 0.1 tile.12
  2.5 11.4 %shard_map.176 = (bf16[4,2,32,1024]{3,2,1,0:T(8,128)(2,1)S(1)}, f32[8,128]{1,0:T(8,128)S(1)}, f32[8,128]{1,0:T(8,128)S(1)}) custom-call(s32[3,8]{1,0:T(4,128)S(1)} %bitcast.14, s32[2,130816]{1,0:T(2,128)} %links_ref.1, f32[256,4,512]{2,1,0:T(4,128)} %gain_ref.1, f32[64,512]{1,0:T(8,128)} %constant.48.clone.p_ref, f32[64,512]{1,0:T(8,128)} %constant.49.clone.q_ref, ...), custom_call_target="tpu_custom_call" | custom-call | tf_op jit(solution)/shard_map/pallas_call | solution.py:199
  13.9 0.0 copy-done.2
  13.9 0.0 copy-done.3
  13.9 0.0 copy-done.6
  13.9 0.0 copy-done
  14.0 0.0 copy-done.1
  14.0 0.0 copy-done.7
  14.0 0.0 copy-done.5
  14.0 0.0 copy-done.4
  14.0 27.9 %shard_map.177 = (f32[8,128]{1,0:T(8,128)S(1)}, f32[4,16,256]{2,1,0:T(8,128)S(1)}) custom-call(bf16[4,2,32,1024]{3,2,1,0:T(8,128)(2,1)S(1)} %get-tuple-element.7.contrib_ref, bf16[128,512]{1,0:T(8,128)(2,1)S(1)} %bitcast.11, bf16[128,512]{1,0:T(8,128)(2,1)S(1)} %bitcast.12, bf16[2,128]{1,0:T(2,128)(2,1)S(1)} %bitcast.15, ...), custom_call_target="tpu_custom_call" | custom-call | tf_op jit(solution)/shard_map/pallas_call | solution.py:547
  41.9 0.7 %constant_dynamic-slice_fusion = f32[8,32]{1,0:T(8,128)} fusion(f32[8,128]{1,0:T(8,128)S(1)} %get-tuple-element.10, s32[]{:T(128)S(6)} %select_n.18), kind=kLoop, calls=%fused_computation.7 | loop fusion | bytes 2052 | tf_op jit(solution)/shard_map/dynamic_slice | solution.py:632
  42.5 0.2 copy.19
  42.8 0.8 %copy.20 = f32[16,1024]{1,0:T(8,128)} copy(f32[16,1024]{0,1:T(8,128)S(1)} %bitcast.17) | data formatting | bytes 131072
  (2 shorter events, 0.0 us)
Async XLA Ops:
  0.6 13.3 %copy-start.2 = (bf16[8,2,32,512]{3,2,1,0:T(8,128)(2,1)S(1)}, bf16[8,2,32,512]{3,2,1,0:T(8,128)(2,1)}, u32[]{:S(2)}) copy-start(bf16[8,2,32,512]{3,2,1,0:T(8,128)(2,1)} %constant.64.table_im_ref) | copy-start | bytes 1572868
  0.6 13.3 %copy-start.3 = (bf16[8,2,32,512]{3,2,1,0:T(8,128)(2,1)S(1)}, bf16[8,2,32,512]{3,2,1,0:T(8,128)(2,1)}, u32[]{:S(2)}) copy-start(bf16[8,2,32,512]{3,2,1,0:T(8,128)(2,1)} %constant.63.table_re_ref) | copy-start | bytes 1572868
  0.7 13.3 %copy-start.6 = (f32[2,512]{1,0:T(2,128)S(1)}, f32[2,512]{1,0:T(2,128)}, u32[]{:S(2)}) copy-start(f32[2,512]{1,0:T(2,128)} %constant.56.clone.chirp_ref) | copy-start | bytes 12292
  0.7 13.3 %copy-start = (bf16[512,1024]{1,0:T(8,128)(2,1)S(1)}, bf16[512,1024]{1,0:T(8,128)(2,1)}, u32[]{:S(2)}) copy-start(bf16[512,1024]{1,0:T(8,128)(2,1)} %constant.55.clone.third_ref) | copy-start | bytes 3145732
  0.7 13.3 %copy-start.1 = (bf16[512,1024]{1,0:T(8,128)(2,1)S(1)}, bf16[512,1024]{1,0:T(8,128)(2,1)}, u32[]{:S(2)}) copy-start(bf16[512,1024]{1,0:T(8,128)(2,1)} %constant.54.clone.second_ref) | copy-start | bytes 3145732
  0.7 13.3 %copy-start.7 = (bf16[1,1,2,128]{3,2,1,0:T(2,128)(2,1)S(1)}, bf16[1,1,2,128]{3,2,1,0:T(2,128)(2,1)}, u32[]{:S(2)}) copy-start(bf16[1,1,2,128]{3,2,1,0:T(2,128)(2,1)} %param.20) | copy-start | bytes 1540
  0.7 13.3 %copy-start.5 = (bf16[1,1,128,512]{3,2,1,0:T(8,128)(2,1)S(1)}, bf16[1,1,128,512]{3,2,1,0:T(8,128)(2,1)}, u32[]{:S(2)}) copy-start(bf16[1,1,128,512]{3,2,1,0:T(8,128)(2,1)} %param.19) | copy-start | bytes 393220
  0.7 13.3 %copy-start.4 = (bf16[1,1,128,512]{3,2,1,0:T(8,128)(2,1)S(1)}, bf16[1,1,128,512]{3,2,1,0:T(8,128)(2,1)}, u32[]{:S(2)}) copy-start(bf16[1,1,128,512]{3,2,1,0:T(8,128)(2,1)} %param.18) | copy-start | bytes 393220

commit v5 on v4

--- a/solution.py
+++ b/solution.py
@@ -245,8 +245,7 @@
     im = np.sin(angle) / math.sqrt(SG)
     blocks = lambda t: t.reshape(SG, FGRID, MC)
     second = np.stack([blocks(re), -blocks(im)], axis=2).reshape(SG, 2 * SG)
-    third = np.stack([blocks(im), blocks(re)], axis=2).reshape(SG, 2 * SG)
-    return [t.astype(jnp.bfloat16) for t in (re, im, second, third)]
+    return [t.astype(jnp.bfloat16) for t in (re, im, second)]
 
 
 def chirp_line():
@@ -312,7 +311,6 @@
     table_re_ref,
     table_im_ref,
     second_ref,
-    third_ref,
     chirp_ref,
     residual_ref,
     grad_ref,
@@ -323,6 +321,7 @@
     left,
     part_out,
     part_in,
+    observed_out,
     observed_in,
     record_out,
     record_in,
@@ -375,6 +374,13 @@
             pl.semaphore_signal(barrier, inc=1, device_id=(z, q, o), device_id_type=mesh_id)
     pl.semaphore_wait(barrier, across_total - 1 + (pols - 1) * owners)
 
+    quarter = observed_ref.shape[1]
+    place = lax.broadcasted_iota(jnp.int32, (2 * NPOL, slots), 1)
+    observed_out[...] = jnp.where(
+        (place >= p * quarter) & (place < (p + 1) * quarter),
+        jnp.concatenate([observed_ref[...]] * pols, axis=1),
+        0.0,
+    )
     copies = []
     for d in range(1, subgrids):
         other = lax.rem(z + d, subgrids)
@@ -391,7 +397,7 @@
         q = lax.rem(p + d, pols)
         observed_copies.append(
             remote(
-                observed_ref, observed_in.at[p], observed_send.at[d], observed_recv.at[d], (z, q, t)
+                observed_out, observed_in.at[p], observed_send.at[d], observed_recv.at[d], (z, q, t)
             )
         )
     for copy in copies + taper_copies + observed_copies:
@@ -399,11 +405,21 @@
 
     table_re = jnp.concatenate([table_re_ref[i, t] for i in range(FGRID)], axis=0)
     table_im = jnp.concatenate([table_im_ref[i, t] for i in range(FGRID)], axis=0)
+
+    turn = jnp.where(
+        lax.broadcasted_iota(jnp.int32, (3 * slots, 2 * MC), 1) < MC, -1.0, 1.0
+    )
 
     def prepare(owner, trail, lead):
         trail3 = chirped_rows(trail, chirp_ref)
         a = jnp.dot(trail3, second_ref[...], preferred_element_type=jnp.float32)
-        b = jnp.dot(trail3, third_ref[...], preferred_element_type=jnp.float32)
+        b = jnp.concatenate(
+            [
+                turn * pltpu.roll(a[:, j * 2 * MC : (j + 1) * 2 * MC], MC, 1)
+                for j in range(a.shape[1] // (2 * MC))
+            ],
+            axis=1,
+        )
         n0, n1, n2 = slice(0, slots), slice(slots, 2 * slots), slice(2 * slots, 3 * slots)
         right[owner, 0:slots, :] = a[n0].astype(jnp.bfloat16)
         right[owner, slots : 2 * slots, :] = (a[n1] - b[n2]).astype(jnp.bfloat16)
@@ -460,7 +476,7 @@
     for copy in part_copies:
         copy.start()
     part_in[plane] = part_out[t]
-    observed_in[p] = observed_ref[...]
+    observed_in[p] = observed_out[...]
     for copy in observed_copies:
         copy.wait()
     observed = observed_in[0]
@@ -506,8 +522,11 @@
     for copy in record_copies:
         copy.start()
     record_in[across] = record_out[...]
-    for k in range(2 * NPOL):
-        residual_ref[k : k + 1, :] = residual[k]
+    rest = jnp.concatenate(residual, axis=0)
+    own_rest = jnp.zeros((2 * NPOL, quarter), jnp.float32)
+    for q in range(pols):
+        own_rest = jnp.where(p == q, rest[:, q * quarter : (q + 1) * quarter], own_rest)
+    residual_ref[...] = own_rest
     for copy in record_copies:
         copy.wait()
 
@@ -547,7 +566,7 @@
     return pl.pallas_call(
         functools.partial(predict_kernel, sizes),
         out_shape=(
-            jax.ShapeDtypeStruct((2 * NPOL, slots), jnp.float32),
+            jax.ShapeDtypeStruct((2 * NPOL, slots // pols), jnp.float32),
             jax.ShapeDtypeStruct((4, own_count, NCH), jnp.float32),
         ),
         in_specs=[vmem] * len(operands),
@@ -560,6 +579,7 @@
             pltpu.VMEM((owners, 4, FGRID * rows, slots), jnp.float32),
             pltpu.VMEM((owners, 8, slots), jnp.float32),
             pltpu.VMEM((plane_total, 8, slots), jnp.float32),
+            pltpu.VMEM((8, slots), jnp.float32),
             pltpu.VMEM((pols, 8, slots), jnp.float32),
             pltpu.VMEM((16, slots), jnp.float32),
             pltpu.VMEM((across_total, 16, slots), jnp.float32),
@@ -595,12 +615,9 @@
     slots = taper_leading_axis.shape[2]
     quarter = measured_correlations.shape[3]
     rows = tile_spectral_lines.shape[3]
-    pol_index = lax.axis_index("pol")
 
     block_table = visibility_groups_table.reshape(3, visibility_groups_table.shape[3])
     observed = measured_correlations.reshape(2 * NPOL, quarter)
-    in_quarter = (jnp.arange(slots, dtype=jnp.int32) // quarter == pol_index)[None, :]
-    observed = jnp.where(in_quarter, jnp.tile(observed, (1, pols)), 0.0)
 
     contrib, gains, idents = fourier(
         tile_spectral_lines[:, 0],
@@ -610,7 +627,7 @@
         antenna_links,
         complex_receiver_factors,
     )
-    table_re, table_im, second, third = [jnp.asarray(t) for t in subgrid_tables()]
+    table_re, table_im, second = [jnp.asarray(t) for t in subgrid_tables()]
     cosine, sine = chirp_line()
     own_count = NST // (subgrids * pols * owners)
     residual, grad = predict(
@@ -626,10 +643,8 @@
         table_re.reshape(FGRID, owners, rows, SG),
         table_im.reshape(FGRID, owners, rows, SG),
         second,
-        third,
         jnp.asarray(np.stack([cosine, sine])),
     )
-    residual = lax.dynamic_slice_in_dim(residual, pol_index * quarter, quarter, 1)
     gain_grad = jnp.transpose(grad, (1, 2, 0)).reshape(own_count, 4 * NCH)
     return residual.reshape(1, 2 * NPOL, 1, quarter), gain_grad
 

time: 43.9 us -> 42.9 us (0.977)
  local copies, waits for them, and re-layouts: 3.47 us -> 2.5 us
    another operation x2 -> x0, local copies, waits for them, and re-layouts: 0.89 us -> none  [on_device(): observed = jnp.where(in_quarter, jnp.tile(observed, (1, pols)), 0.0)]
    dynamic_slice x1 -> x0, local copies, waits for them, and re-layouts: 0.67 us -> none  [on_device(): lax.dynamic_slice_in_dim(residual, pol_index * quarter, quarter, 1)]
    unnamed x18 -> x19, local copies, waits for them, and re-layouts: 1.68 us -> 2.27 us
where the time goes in v5:
time: 42.9 us; the launch traced here: 42.6 us
  Pallas kernels  39.4 us (92%)
  local copies, waits for them, and re-layouts  2.5 us (6%)
  between operations  0.78 us (2%)
    pallas_call x1, Pallas kernels, predict(): pl.pallas_call(functools.partial(predict_kernel, sizes), out_shape=(jax.S...  27.9 us
    pallas_call x1, Pallas kernels, fourier(): pl.pallas_call(fourier_kernel, out_shape=(jax.ShapeDtypeStruct(out, jnp.b...  11.4 us
    unnamed x19, local copies, waits for them, and re-layouts  2.27 us

profile of v5, /device:TPU:0, one launch (start us, length us, event | category | flops | bytes accessed | tf_op | source)
XLA Modules:
  0.0 42.6 jit_solution(6567580885865802895)
XLA Ops:
  0.6 0.0 copy-start.1
  0.6 0.0 copy-start.2
  0.7 0.0 copy-start.6
  0.7 0.0 copy-start
  0.7 0.0 copy-start.5
  0.7 0.0 copy-start.7
  0.7 0.0 copy-start.4
  0.7 0.0 copy-start.3
  0.7 0.8 %copy.24 = s32[1,1,3,8]{3,2,1,0:T(4,128)S(1)} copy(s32[1,1,3,8]{3,1,2,0:T(1,128)} %param.21) | data formatting | bytes 192
  1.6 11.4 %shard_map.167 = (bf16[4,2,32,1024]{3,2,1,0:T(8,128)(2,1)S(1)}, f32[8,128]{1,0:T(8,128)S(1)}, f32[8,128]{1,0:T(8,128)S(1)}) custom-call(s32[3,8]{1,0:T(4,128)S(1)} %bitcast.16, s32[2,130816]{1,0:T(2,128)} %links_ref.1, f32[256,4,512]{2,1,0:T(4,128)} %gain_ref.1, f32[64,512]{1,0:T(8,128)} %constant.16.clone.p_ref, f32[64,512]{1,0:T(8,128)} %constant.17.clone.q_ref, ...), custom_call_target="tpu_custom_call" | custom-call | tf_op jit(solution)/shard_map/pallas_call | solution.py:199
  13.0 0.0 copy-done.1
  13.0 0.0 copy-done.2
  13.0 0.0 copy-done.6
  13.0 0.0 copy-done
  13.0 0.0 copy-done.5
  13.0 0.0 copy-done.7
  13.0 0.0 copy-done.4
  13.1 0.0 copy-done.3
  13.1 27.9 %shard_map.168 = (f32[8,32]{1,0:T(8,128)S(1)}, f32[4,16,256]{2,1,0:T(8,128)S(1)}) custom-call(bf16[4,2,32,1024]{3,2,1,0:T(8,128)(2,1)S(1)} %get-tuple-element.7.contrib_ref, bf16[128,512]{1,0:T(8,128)(2,1)S(1)} %bitcast.13, bf16[128,512]{1,0:T(8,128)(2,1)S(1)} %bitcast.14, bf16[2,128]{1,0:T(2,128)(2,1)S(1)} %bitcast.19, f32[8,32]{1,0:T(8,128)S(1)} %bitcast.17, ...), custom_call_target="tpu_custom_call" | custom-call | tf_op jit(solution)/shard_map/pallas_call | solution.py:566
  41.0 0.2 copy.19
  41.3 0.8 %copy.21 = f32[16,1024]{1,0:T(8,128)} copy(f32[16,1024]{0,1:T(8,128)S(1)} %bitcast.21) | data formatting | bytes 131072
  42.1 0.6 %copy.26 = f32[1,8,1,32]{3,2,1,0:T(1,128)} copy(f32[1,8,1,32]{3,2,1,0:T(1,128)S(1)} %bitcast.18) | data formatting | bytes 2048
Async XLA Ops:
  0.6 12.4 %copy-start.1 = (bf16[8,2,32,512]{3,2,1,0:T(8,128)(2,1)S(1)}, bf16[8,2,32,512]{3,2,1,0:T(8,128)(2,1)}, u32[]{:S(2)}) copy-start(bf16[8,2,32,512]{3,2,1,0:T(8,128)(2,1)} %constant.31.table_im_ref) | copy-start | bytes 1572868
  0.6 12.4 %copy-start.2 = (bf16[8,2,32,512]{3,2,1,0:T(8,128)(2,1)S(1)}, bf16[8,2,32,512]{3,2,1,0:T(8,128)(2,1)}, u32[]{:S(2)}) copy-start(bf16[8,2,32,512]{3,2,1,0:T(8,128)(2,1)} %constant.30.table_re_ref) | copy-start | bytes 1572868
  0.7 12.4 %copy-start.6 = (f32[2,512]{1,0:T(2,128)S(1)}, f32[2,512]{1,0:T(2,128)}, u32[]{:S(2)}) copy-start(f32[2,512]{1,0:T(2,128)} %constant.23.clone.chirp_ref) | copy-start | bytes 12292
  0.7 12.4 %copy-start = (bf16[512,1024]{1,0:T(8,128)(2,1)S(1)}, bf16[512,1024]{1,0:T(8,128)(2,1)}, u32[]{:S(2)}) copy-start(bf16[512,1024]{1,0:T(8,128)(2,1)} %constant.22.clone.second_ref) | copy-start | bytes 3145732
  0.7 12.3 %copy-start.5 = (f32[1,8,1,32]{3,2,1,0:T(1,128)S(1)}, f32[1,8,1,32]{3,2,1,0:T(1,128)}, u32[]{:S(2)}) copy-start(f32[1,8,1,32]{3,2,1,0:T(1,128)} %param.20) | copy-start | bytes 3076
  0.7 12.3 %copy-start.7 = (bf16[1,1,2,128]{3,2,1,0:T(2,128)(2,1)S(1)}, bf16[1,1,2,128]{3,2,1,0:T(2,128)(2,1)}, u32[]{:S(2)}) copy-start(bf16[1,1,2,128]{3,2,1,0:T(2,128)(2,1)} %param.19) | copy-start | bytes 1540
  0.7 12.3 %copy-start.4 = (bf16[1,1,128,512]{3,2,1,0:T(8,128)(2,1)S(1)}, bf16[1,1,128,512]{3,2,1,0:T(8,128)(2,1)}, u32[]{:S(2)}) copy-start(bf16[1,1,128,512]{3,2,1,0:T(8,128)(2,1)} %param.18) | copy-start | bytes 393220
  0.7 12.3 %copy-start.3 = (bf16[1,1,128,512]{3,2,1,0:T(8,128)(2,1)S(1)}, bf16[1,1,128,512]{3,2,1,0:T(8,128)(2,1)}, u32[]{:S(2)}) copy-start(bf16[1,1,128,512]{3,2,1,0:T(8,128)(2,1)} %param.17) | copy-start | bytes 393220

commit v6 on v5

--- a/solution.py
+++ b/solution.py
@@ -17,7 +17,7 @@
 NW = 2
 NCH = 256
 NST = 512
-CHUNK = 512
+CHUNK = 1024
 
 w_chirp = 0.37
 grad_scale = 0.1
@@ -382,7 +382,7 @@
         0.0,
     )
     copies = []
-    for d in range(1, subgrids):
+    for d in sorted(range(1, subgrids), key=lambda d: -min(d, subgrids - d)):
         other = lax.rem(z + d, subgrids)
         copies.append(
             remote(contrib_ref.at[other], got.at[z], got_send.at[d], got_recv.at[d], (other, p, t))

time: 42.9 us -> 39.5 us (0.921)
  Pallas kernels: 39.4 us -> 36.1 us
    pallas_call x1, Pallas kernels: 11.4 us -> 9.04 us  [fourier(): pl.pallas_call(fourier_kernel, out_shape=(jax.ShapeDtypeStruct(out, jnp.b...]
    pallas_call x1, Pallas kernels: 27.9 us -> 27 us  [predict(): pl.pallas_call(functools.partial(predict_kernel, sizes), out_shape=(jax.S...]
where the time goes in v6:
time: 39.5 us; the launch traced here: 39.3 us
  Pallas kernels  36.1 us (91%)
  local copies, waits for them, and re-layouts  2.5 us (6%)
  between operations  0.78 us (2%)
    pallas_call x1, Pallas kernels, predict(): pl.pallas_call(functools.partial(predict_kernel, sizes), out_shape=(jax.S...  27 us
    pallas_call x1, Pallas kernels, fourier(): pl.pallas_call(fourier_kernel, out_shape=(jax.ShapeDtypeStruct(out, jnp.b...  9.04 us
    unnamed x19, local copies, waits for them, and re-layouts  2.27 us

profile of v6, /device:TPU:0, one launch (start us, length us, event | category | flops | bytes accessed | tf_op | source)
XLA Modules:
  0.0 39.3 jit_solution(6268425656945700689)
XLA Ops:
  0.6 0.0 copy-start.1
  0.6 0.0 copy-start.2
  0.7 0.0 copy-start.6
  0.7 0.0 copy-start
  0.7 0.0 copy-start.5
  0.7 0.0 copy-start.7
  0.7 0.0 copy-start.4
  0.7 0.0 copy-start.3
  0.7 0.8 %copy.24 = s32[1,1,3,8]{3,2,1,0:T(4,128)S(1)} copy(s32[1,1,3,8]{3,1,2,0:T(1,128)} %param.21) | data formatting | bytes 192
  1.6 9.0 %shard_map.167 = (bf16[4,2,32,1024]{3,2,1,0:T(8,128)(2,1)S(1)}, f32[8,128]{1,0:T(8,128)S(1)}, f32[8,128]{1,0:T(8,128)S(1)}) custom-call(s32[3,8]{1,0:T(4,128)S(1)} %bitcast.16, s32[2,130816]{1,0:T(2,128)} %links_ref.1, f32[256,4,512]{2,1,0:T(4,128)} %gain_ref.1, f32[64,512]{1,0:T(8,128)} %constant.16.clone.p_ref, f32[64,512]{1,0:T(8,128)} %constant.17.clone.q_ref, ...), custom_call_target="tpu_custom_call" | custom-call | tf_op jit(solution)/shard_map/pallas_call | solution.py:199
  10.6 0.0 copy-done.1
  10.6 0.0 copy-done.2
  10.6 0.0 copy-done.6
  10.6 0.0 copy-done
  10.6 0.0 copy-done.5
  10.6 0.0 copy-done.7
  10.7 0.0 copy-done.4
  10.7 0.0 copy-done.3
  10.7 27.0 %shard_map.168 = (f32[8,32]{1,0:T(8,128)S(1)}, f32[4,16,256]{2,1,0:T(8,128)S(1)}) custom-call(bf16[4,2,32,1024]{3,2,1,0:T(8,128)(2,1)S(1)} %get-tuple-element.7.contrib_ref, bf16[128,512]{1,0:T(8,128)(2,1)S(1)} %bitcast.13, bf16[128,512]{1,0:T(8,128)(2,1)S(1)} %bitcast.14, bf16[2,128]{1,0:T(2,128)(2,1)S(1)} %bitcast.19, f32[8,32]{1,0:T(8,128)S(1)} %bitcast.17, ...), custom_call_target="tpu_custom_call" | custom-call | tf_op jit(solution)/shard_map/pallas_call | solution.py:566
  37.7 0.2 copy.19
  37.9 0.8 %copy.21 = f32[16,1024]{1,0:T(8,128)} copy(f32[16,1024]{0,1:T(8,128)S(1)} %bitcast.21) | data formatting | bytes 131072
  38.8 0.6 %copy.26 = f32[1,8,1,32]{3,2,1,0:T(1,128)} copy(f32[1,8,1,32]{3,2,1,0:T(1,128)S(1)} %bitcast.18) | data formatting | bytes 2048
Async XLA Ops:
  0.6 10.0 %copy-start.1 = (bf16[8,2,32,512]{3,2,1,0:T(8,128)(2,1)S(1)}, bf16[8,2,32,512]{3,2,1,0:T(8,128)(2,1)}, u32[]{:S(2)}) copy-start(bf16[8,2,32,512]{3,2,1,0:T(8,128)(2,1)} %constant.31.table_im_ref) | copy-start | bytes 1572868
  0.6 10.0 %copy-start.2 = (bf16[8,2,32,512]{3,2,1,0:T(8,128)(2,1)S(1)}, bf16[8,2,32,512]{3,2,1,0:T(8,128)(2,1)}, u32[]{:S(2)}) copy-start(bf16[8,2,32,512]{3,2,1,0:T(8,128)(2,1)} %constant.30.table_re_ref) | copy-start | bytes 1572868
  0.7 10.0 %copy-start.6 = (f32[2,512]{1,0:T(2,128)S(1)}, f32[2,512]{1,0:T(2,128)}, u32[]{:S(2)}) copy-start(f32[2,512]{1,0:T(2,128)} %constant.23.clone.chirp_ref) | copy-start | bytes 12292
  0.7 10.0 %copy-start = (bf16[512,1024]{1,0:T(8,128)(2,1)S(1)}, bf16[512,1024]{1,0:T(8,128)(2,1)}, u32[]{:S(2)}) copy-start(bf16[512,1024]{1,0:T(8,128)(2,1)} %constant.22.clone.second_ref) | copy-start | bytes 3145732
  0.7 10.0 %copy-start.5 = (f32[1,8,1,32]{3,2,1,0:T(1,128)S(1)}, f32[1,8,1,32]{3,2,1,0:T(1,128)}, u32[]{:S(2)}) copy-start(f32[1,8,1,32]{3,2,1,0:T(1,128)} %param.20) | copy-start | bytes 3076
  0.7 10.0 %copy-start.7 = (bf16[1,1,2,128]{3,2,1,0:T(2,128)(2,1)S(1)}, bf16[1,1,2,128]{3,2,1,0:T(2,128)(2,1)}, u32[]{:S(2)}) copy-start(bf16[1,1,2,128]{3,2,1,0:T(2,128)(2,1)} %param.19) | copy-start | bytes 1540
  0.7 10.0 %copy-start.4 = (bf16[1,1,128,512]{3,2,1,0:T(8,128)(2,1)S(1)}, bf16[1,1,128,512]{3,2,1,0:T(8,128)(2,1)}, u32[]{:S(2)}) copy-start(bf16[1,1,128,512]{3,2,1,0:T(8,128)(2,1)} %param.18) | copy-start | bytes 393220
  0.7 10.0 %copy-start.3 = (bf16[1,1,128,512]{3,2,1,0:T(8,128)(2,1)S(1)}, bf16[1,1,128,512]{3,2,1,0:T(8,128)(2,1)}, u32[]{:S(2)}) copy-start(bf16[1,1,128,512]{3,2,1,0:T(8,128)(2,1)} %param.17) | copy-start | bytes 393220
